TPU v7x, 32 devices: a whole 2x2x4 slice. The times are simulated.
32 devices in a mesh: dp: 2 (over y), gx: 4 (over z), gy: 4 (over x, core).
Axes of the slice: x: 2, y: 2, z: 4, core: 2. Of those that a mesh axis runs over, the one named last changes fastest.
Arguments:
- block_input: bfloat16 [3, 2, 2048, 1280], P(None, 'dp', ('gx', 'gy')), may hold values from -6 to 6
- picture: int32 [3, 2, 2048], P(None, 'dp'), may hold values from 0 to 24, as said below
- position: int32 [2, 3, 2, 2048], P(None, None, 'dp'), may hold values from 0 to 31, as said below
- patch_mask: int32 [3, 2, 2048], P(None, 'dp'), may hold values from 0 to 1, as said below
- gain_attn: float32 [1280], replicated, may hold values from 0.5 to 1.5
- shift_attn: float32 [1280], replicated, may hold values from -3 to 3
- w_query: bfloat16 [1280, 1280], P(('dp', 'gx'), 'gy'), may hold values from -0.15625 to 0.15625
- b_query: float32 [1280], replicated, may hold values from -3 to 3
- w_key: bfloat16 [1280, 1280], P(('dp', 'gx'), 'gy'), may hold values from -0.15625 to 0.15625
- b_key: float32 [1280], replicated, may hold values from -3 to 3
- w_value: bfloat16 [1280, 1280], P(('dp', 'gx'), 'gy'), may hold values from -0.15625 to 0.15625
- b_value: float32 [1280], replicated, may hold values from -3 to 3
- w_out: bfloat16 [1280, 1280], P(('dp', 'gx'), 'gy'), may hold values from -1.25 to 1.25
- b_out: float32 [1280], replicated, may hold values from -3 to 3
- gain_mlp: float32 [1280], replicated, may hold values from 0.5 to 1.5
- shift_mlp: float32 [1280], replicated, may hold values from -3 to 3
- w_up: bfloat16 [1280, 5120], P(('dp', 'gx'), 'gy'), may hold values from -0.15625 to 0.15625
- b_up: float32 [5120], replicated, may hold values from -3 to 3
- w_down: bfloat16 [1280, 5120], P(('dp', 'gx'), 'gy'), may hold values from -0.15625 to 0.15625
- b_down: float32 [1280], replicated, may hold values from -3 to 3
- out_grad: bfloat16 [3, 2, 2048, 1280], P(None, 'dp', ('gx', 'gy')), may hold values from -6 to 6
Outputs:
- block_output: bfloat16 [3, 2, 2048, 1280], P(None, 'dp', ('gx', 'gy'))
- input_grad: float32 [3, 2, 2048, 1280], P(None, 'dp', ('gx', 'gy'))
- gain_attn_grad: float32 [1280], replicated
- shift_attn_grad: float32 [1280], replicated
- w_query_grad: float32 [1280, 1280], P(('dp', 'gx'), 'gy')
- b_query_grad: float32 [1280], replicated
- w_key_grad: float32 [1280, 1280], P(('dp', 'gx'), 'gy')
- b_key_grad: float32 [1280], replicated
- w_value_grad: float32 [1280, 1280], P(('dp', 'gx'), 'gy')
- b_value_grad: float32 [1280], replicated
- w_out_grad: float32 [1280, 1280], P(('dp', 'gx'), 'gy')
- b_out_grad: float32 [1280], replicated
- gain_mlp_grad: float32 [1280], replicated
- shift_mlp_grad: float32 [1280], replicated
- w_up_grad: float32 [1280, 5120], P(('dp', 'gx'), 'gy')
- b_up_grad: float32 [5120], replicated
- w_down_grad: float32 [1280, 5120], P(('dp', 'gx'), 'gy')
- b_down_grad: float32 [1280], replicated
Inputs may be any that keep to these rules, and one draw needn't show every extreme that they name: Each row holds whole pictures one after another from slot 0, numbered 0, 1, 2, ... in that order; every picture has h by w patches, one of each row 32 by 32 and the others with sides from 10 to 31; the slots after the last picture, at least one a row, hold 24. position[0] and position[1] are the row and column of a patch within its picture, in row-major order; padding slots hold 0. `patch_mask`: 1 on the slots of pictures, 0 on the padding after them.
All inputs are finite; a program needn't handle non-finite values.
Results may differ from a plain program's by a relative error of at most 0.02.
Values may be sent and summed in bfloat16 or wider, within the bound.
No kernel may reach another device: no remote copies, remote signals or barrier semaphores. Data moves between devices by JAX's collectives and lax.ppermute only.
A program may use at most 144 MiB of HBM per device.

v0:
```python
import jax
import jax.numpy as jnp
from jax import lax
from jax.sharding import PartitionSpec as P

HEAD_DIM = 80


EPSILON = 1e-06


def layer_norm(values, norm_gain, norm_shift):
    center = values - jnp.mean(values, axis=-1, keepdims=True)
    factor = lax.rsqrt(jnp.mean(center * center, axis=-1, keepdims=True) + EPSILON)
    normal = center * factor
    return (normal * norm_gain + norm_shift, normal, factor)


def norm_back(upstream, normal, factor, norm_gain):
    shaped = upstream * norm_gain
    first_mean = jnp.mean(shaped, axis=-1, keepdims=True)
    second_mean = jnp.mean(shaped * normal, axis=-1, keepdims=True)
    return factor * (shaped - first_mean - normal * second_mean)


def rotary_tables(position_rows, first_slot, slot_total):
    quarter = HEAD_DIM // 4
    inverse = 10000.0 ** (-jnp.arange(quarter, dtype=jnp.float32) / quarter)
    picked = lax.dynamic_slice_in_dim(position_rows, first_slot, slot_total, 2).astype(jnp.float32)
    along_rows = jnp.transpose(picked[0])[:, :, None] * inverse
    along_cols = jnp.transpose(picked[1])[:, :, None] * inverse
    angles = jnp.concatenate([along_rows, along_cols, along_rows, along_cols], axis=-1)[
        :, :, None, :
    ]
    return (jnp.cos(angles), jnp.sin(angles))


def rotate(values, cos_table, sin_table):
    halfway = HEAD_DIM // 2
    turned = jnp.concatenate([-values[..., halfway:], values[..., :halfway]], axis=-1)
    return values * cos_table + turned * sin_table


def rotate_back(upstream, cos_table, sin_table):
    halfway = HEAD_DIM // 2
    moved = upstream * sin_table
    return upstream * cos_table + jnp.concatenate(
        [moved[..., halfway:], -moved[..., :halfway]], axis=-1
    )


def attention_scores(queries, keys_all, visible):
    raw = jnp.einsum(
        "qrhd,krhd->rhqk", queries, keys_all, preferred_element_type=jnp.float32
    ) * HEAD_DIM ** (-0.5)
    return jnp.where(visible[:, None], raw, -1e30)


def per_device(
    block_input,
    picture,
    position,
    patch_mask,
    gain_attn,
    shift_attn,
    w_query,
    b_query,
    w_key,
    b_key,
    w_value,
    b_value,
    w_out,
    b_out,
    gain_mlp,
    shift_mlp,
    w_up,
    b_up,
    w_down,
    b_down,
    out_grad,
):
    across = lax.axis_size("gy")
    column = lax.axis_index("gy")
    segment = lax.axis_index("gx")
    micro_count = block_input.shape[0]
    row_count = block_input.shape[1]
    own_rows = block_input.shape[2]
    slot_count = picture.shape[2]
    query_rows = own_rows * across
    head_cols = w_query.shape[1]
    hidden_cols = w_up.shape[1]
    heads_here = head_cols // HEAD_DIM
    query_start = segment * query_rows
    head_start = column * head_cols
    up_start = column * hidden_cols
    scaling = HEAD_DIM ** (-0.5)
    query_bias = lax.dynamic_slice_in_dim(b_query, head_start, head_cols)
    key_bias = lax.dynamic_slice_in_dim(b_key, head_start, head_cols)
    value_bias = lax.dynamic_slice_in_dim(b_value, head_start, head_cols)
    up_bias = lax.dynamic_slice_in_dim(b_up, up_start, hidden_cols)
    head_shape = (query_rows, row_count, heads_here, HEAD_DIM)
    grad_shards = [
        jnp.zeros(shard.shape, jnp.float32)
        for shard in (w_query, w_key, w_value, w_out, w_up, w_down)
    ]
    sum_gain_attn = jnp.zeros(gain_attn.shape, jnp.float32)
    sum_shift_attn = jnp.zeros(gain_attn.shape, jnp.float32)
    sum_query_bias = jnp.zeros((head_cols,), jnp.float32)
    sum_key_bias = jnp.zeros((head_cols,), jnp.float32)
    sum_value_bias = jnp.zeros((head_cols,), jnp.float32)
    sum_out_bias = jnp.zeros(b_out.shape, jnp.float32)
    sum_gain_mlp = jnp.zeros(gain_mlp.shape, jnp.float32)
    sum_shift_mlp = jnp.zeros(gain_mlp.shape, jnp.float32)
    sum_up_bias = jnp.zeros((hidden_cols,), jnp.float32)
    sum_down_bias = jnp.zeros(b_down.shape, jnp.float32)
    outputs = []
    input_grads = []
    for micro in range(micro_count):
        blocks = (
            lax.all_gather(w_query, ("dp", "gx"), axis=0, tiled=True),
            lax.all_gather(w_key, ("dp", "gx"), axis=0, tiled=True),
            lax.all_gather(w_value, ("dp", "gx"), axis=0, tiled=True),
            lax.all_gather(w_out, ("dp", "gx"), axis=0, tiled=True),
            lax.all_gather(w_up, ("dp", "gx"), axis=0, tiled=True),
            lax.all_gather(w_down, ("dp", "gx"), axis=0, tiled=True),
        )
        full_query, full_key, full_value, full_out, full_up, full_down = blocks
        inputs = jnp.transpose(block_input[micro], (1, 0, 2)).astype(jnp.float32)
        normed, normal_one, factor_one = layer_norm(inputs, gain_attn, shift_attn)
        normed_rows = lax.all_gather(normed.astype(jnp.bfloat16), "gy", axis=0, tiled=True)
        cos_table, sin_table = rotary_tables(position[:, micro], query_start, query_rows)
        query_pre = (
            jnp.einsum("srd,dc->src", normed_rows, full_query, preferred_element_type=jnp.float32)
            + query_bias
        )
        key_pre = (
            jnp.einsum("srd,dc->src", normed_rows, full_key, preferred_element_type=jnp.float32)
            + key_bias
        )
        value_pre = (
            jnp.einsum("srd,dc->src", normed_rows, full_value, preferred_element_type=jnp.float32)
            + value_bias
        )
        queries = rotate(query_pre.reshape(head_shape), cos_table, sin_table).astype(jnp.bfloat16)
        key_here = rotate(key_pre.reshape(head_shape), cos_table, sin_table).astype(jnp.bfloat16)
        value_here = value_pre.reshape(head_shape).astype(jnp.bfloat16)
        keys_all, values_all = (
            lax.all_gather(key_here, "gx", axis=0, tiled=True),
            lax.all_gather(value_here, "gx", axis=0, tiled=True),
        )
        picture_row = picture[micro]
        query_picture = lax.dynamic_slice_in_dim(picture_row, query_start, query_rows, 1)
        query_places = query_start + jnp.arange(query_rows)
        same_picture = (query_picture[:, :, None] == picture_row[:, None, :]) & (
            patch_mask[micro][:, None, :] == 1
        )
        itself = (query_places[:, None] == jnp.arange(slot_count)[None, :])[None]
        visible = same_picture | itself
        scores = attention_scores(queries, keys_all, visible)
        highest = jnp.max(scores, axis=-1, keepdims=True)
        raised = jnp.exp(scores - highest)
        summed = jnp.sum(raised, axis=-1, keepdims=True)
        log_total = highest + jnp.log(summed)
        attend = (raised / summed).astype(jnp.bfloat16)
        mixture = jnp.einsum(
            "rhqk,krhd->qrhd", attend, values_all, preferred_element_type=jnp.float32
        )
        mixture = mixture.reshape(query_rows, row_count, head_cols).astype(jnp.bfloat16)
        branch = (
            lax.psum_scatter(
                jnp.einsum("srh,oh->sro", mixture, full_out, preferred_element_type=jnp.float32),
                "gy",
                scatter_dimension=0,
                tiled=True,
            )
            + b_out
        )
        middle = inputs + branch
        normed_two, normal_two, factor_two = layer_norm(middle, gain_mlp, shift_mlp)
        mlp_rows = lax.all_gather(normed_two.astype(jnp.bfloat16), "gy", axis=0, tiled=True)
        hidden = (
            jnp.einsum("srd,df->srf", mlp_rows, full_up, preferred_element_type=jnp.float32)
            + up_bias
        )
        squashed = jax.nn.sigmoid(1.702 * hidden)
        active = (hidden * squashed).astype(jnp.bfloat16)
        result = (
            lax.psum_scatter(
                jnp.einsum(
                    "srf,of->sro", active, full_down, preferred_element_type=jnp.float32
                ).astype(jnp.bfloat16),
                "gy",
                scatter_dimension=0,
                tiled=True,
            ).astype(jnp.float32)
            + b_down
        )
        outputs.append(jnp.transpose(middle + result, (1, 0, 2)).astype(jnp.bfloat16))
        cotangent = jnp.transpose(out_grad[micro], (1, 0, 2))
        sum_down_bias = sum_down_bias + jnp.sum(cotangent.astype(jnp.float32), axis=(0, 1))
        cot_rows = lax.all_gather(cotangent, "gy", axis=0, tiled=True)
        grad_down = jnp.einsum("srd,srf->df", cot_rows, active, preferred_element_type=jnp.float32)
        active_grad = jnp.einsum(
            "srd,df->srf", cot_rows, full_down, preferred_element_type=jnp.float32
        )
        hidden_grad = (
            active_grad * (squashed + 1.702 * hidden * squashed * (1.0 - squashed))
        ).astype(jnp.bfloat16)
        sum_up_bias = sum_up_bias + jnp.sum(hidden_grad.astype(jnp.float32), axis=(0, 1))
        grad_up = jnp.einsum(
            "srd,srf->df", mlp_rows, hidden_grad, preferred_element_type=jnp.float32
        )
        normed_two_grad = lax.psum_scatter(
            jnp.einsum("srf,df->srd", hidden_grad, full_up, preferred_element_type=jnp.float32),
            "gy",
            scatter_dimension=0,
            tiled=True,
        )
        sum_gain_mlp = sum_gain_mlp + jnp.sum(normed_two_grad * normal_two, axis=(0, 1))
        sum_shift_mlp = sum_shift_mlp + jnp.sum(normed_two_grad, axis=(0, 1))
        middle_grad = cotangent.astype(jnp.float32) + norm_back(
            normed_two_grad, normal_two, factor_two, gain_mlp
        )
        branch_grad = middle_grad.astype(jnp.bfloat16)
        sum_out_bias = sum_out_bias + jnp.sum(branch_grad.astype(jnp.float32), axis=(0, 1))
        branch_rows = lax.all_gather(branch_grad, "gy", axis=0, tiled=True)
        grad_out = jnp.einsum(
            "srd,srh->dh", branch_rows, mixture, preferred_element_type=jnp.float32
        )
        mixture_grad = jnp.einsum(
            "srd,dh->srh", branch_rows, full_out, preferred_element_type=jnp.float32
        )
        mixture_grad = mixture_grad.astype(jnp.bfloat16).reshape(head_shape)
        again = jnp.exp(attention_scores(queries, keys_all, visible) - log_total)
        again_low = again.astype(jnp.bfloat16)
        attend_grad = jnp.einsum(
            "qrhd,krhd->rhqk", mixture_grad, values_all, preferred_element_type=jnp.float32
        )
        score_grad = (
            again * (attend_grad - jnp.sum(again * attend_grad, axis=-1, keepdims=True))
        ).astype(jnp.bfloat16)
        query_grad = (
            jnp.einsum("rhqk,krhd->qrhd", score_grad, keys_all, preferred_element_type=jnp.float32)
            * scaling
        )
        key_part = (
            jnp.einsum("rhqk,qrhd->krhd", score_grad, queries, preferred_element_type=jnp.float32)
            * scaling
        )
        value_part = jnp.einsum(
            "rhqk,qrhd->krhd", again_low, mixture_grad, preferred_element_type=jnp.float32
        )
        key_grad, value_grad = (
            lax.psum_scatter(key_part, "gx", scatter_dimension=0, tiled=True),
            lax.psum_scatter(value_part, "gx", scatter_dimension=0, tiled=True),
        )
        flat_shape = (query_rows, row_count, head_cols)
        query_pre_grad = (
            rotate_back(query_grad, cos_table, sin_table).reshape(flat_shape).astype(jnp.bfloat16)
        )
        key_pre_grad = (
            rotate_back(key_grad, cos_table, sin_table).reshape(flat_shape).astype(jnp.bfloat16)
        )
        value_pre_grad = value_grad.reshape(flat_shape).astype(jnp.bfloat16)
        sum_query_bias = sum_query_bias + jnp.sum(query_pre_grad.astype(jnp.float32), axis=(0, 1))
        sum_key_bias = sum_key_bias + jnp.sum(key_pre_grad.astype(jnp.float32), axis=(0, 1))
        sum_value_bias = sum_value_bias + jnp.sum(value_pre_grad.astype(jnp.float32), axis=(0, 1))
        grad_query = jnp.einsum(
            "srd,src->dc", normed_rows, query_pre_grad, preferred_element_type=jnp.float32
        )
        grad_key = jnp.einsum(
            "srd,src->dc", normed_rows, key_pre_grad, preferred_element_type=jnp.float32
        )
        grad_value = jnp.einsum(
            "srd,src->dc", normed_rows, value_pre_grad, preferred_element_type=jnp.float32
        )
        from_query = jnp.einsum(
            "src,dc->srd", query_pre_grad, full_query, preferred_element_type=jnp.float32
        )
        from_key = jnp.einsum(
            "src,dc->srd", key_pre_grad, full_key, preferred_element_type=jnp.float32
        )
        from_value = jnp.einsum(
            "src,dc->srd", value_pre_grad, full_value, preferred_element_type=jnp.float32
        )
        normed_grad = lax.psum_scatter(
            (from_query + from_key + from_value).astype(jnp.bfloat16),
            "gy",
            scatter_dimension=0,
            tiled=True,
        ).astype(jnp.float32)
        sum_gain_attn = sum_gain_attn + jnp.sum(normed_grad * normal_one, axis=(0, 1))
        sum_shift_attn = sum_shift_attn + jnp.sum(normed_grad, axis=(0, 1))
        input_grad = middle_grad + norm_back(normed_grad, normal_one, factor_one, gain_attn)
        input_grads.append(jnp.transpose(input_grad, (1, 0, 2)))
        reduced = (
            lax.psum_scatter(grad_query, ("dp", "gx"), scatter_dimension=0, tiled=True),
            lax.psum_scatter(grad_key, ("dp", "gx"), scatter_dimension=0, tiled=True),
            lax.psum_scatter(grad_value, ("dp", "gx"), scatter_dimension=0, tiled=True),
            lax.psum_scatter(grad_out, ("dp", "gx"), scatter_dimension=0, tiled=True),
            lax.psum_scatter(grad_up, ("dp", "gx"), scatter_dimension=0, tiled=True),
            lax.psum_scatter(grad_down, ("dp", "gx"), scatter_dimension=0, tiled=True),
        )
        grad_shards = [held + fresh for held, fresh in zip(grad_shards, reduced)]
    query_bias_full = lax.dynamic_update_slice_in_dim(
        jnp.zeros(b_query.shape, jnp.float32), sum_query_bias, head_start, 0
    )
    key_bias_full = lax.dynamic_update_slice_in_dim(
        jnp.zeros(b_key.shape, jnp.float32), sum_key_bias, head_start, 0
    )
    value_bias_full = lax.dynamic_update_slice_in_dim(
        jnp.zeros(b_value.shape, jnp.float32), sum_value_bias, head_start, 0
    )
    up_bias_full = lax.dynamic_update_slice_in_dim(
        jnp.zeros(b_up.shape, jnp.float32), sum_up_bias, up_start, 0
    )
    vectors = lax.psum(
        (
            sum_gain_attn,
            sum_shift_attn,
            query_bias_full,
            key_bias_full,
            value_bias_full,
            sum_out_bias,
            sum_gain_mlp,
            sum_shift_mlp,
            up_bias_full,
            sum_down_bias,
        ),
        ("dp", "gx", "gy"),
    )
    block_output = jnp.stack(outputs)
    input_grad_all = jnp.stack(input_grads)
    return (
        block_output,
        input_grad_all,
        vectors[0],
        vectors[1],
        grad_shards[0],
        vectors[2],
        grad_shards[1],
        vectors[3],
        grad_shards[2],
        vectors[4],
        grad_shards[3],
        vectors[5],
        vectors[6],
        vectors[7],
        grad_shards[4],
        vectors[8],
        grad_shards[5],
        vectors[9],
    )


def solution(mesh):
    placed = (
        P(None, "dp", ("gx", "gy"), None),
        P(None, "dp", None),
        P(None, None, "dp", None),
        P(None, "dp", None),
        P(),
        P(),
        P(("dp", "gx"), "gy"),
        P(),
        P(("dp", "gx"), "gy"),
        P(),
        P(("dp", "gx"), "gy"),
        P(),
        P(("dp", "gx"), "gy"),
        P(),
        P(),
        P(),
        P(("dp", "gx"), "gy"),
        P(),
        P(("dp", "gx"), "gy"),
        P(),
        P(None, "dp", ("gx", "gy"), None),
    )
    return jax.shard_map(
        per_device,
        mesh=mesh,
        in_specs=placed,
        out_specs=(
            P(None, "dp", ("gx", "gy"), None),
            P(None, "dp", ("gx", "gy"), None),
            P(),
            P(),
            P(("dp", "gx"), "gy"),
            P(),
            P(("dp", "gx"), "gy"),
            P(),
            P(("dp", "gx"), "gy"),
            P(),
            P(("dp", "gx"), "gy"),
            P(),
            P(),
            P(),
            P(("dp", "gx"), "gy"),
            P(),
            P(("dp", "gx"), "gy"),
            P(),
        ),
        check_vma=False,
    )
```

profile of v0, /device:TPU:0, one launch (start us, length us, event | category | flops | bytes accessed | tf_op | source)
XLA Modules:
  0.0 1798.1 jit_solution(1486802666801768990)
XLA Ops:
  16.6 36.7 %all_gather.88 = bf16[1280,320]{1,0:T(8,128)(2,1)S(1)} all-gather(bf16[160,320]{1,0:T(8,128)(2,1)S(1)} %copy-done.107), channel_id=1, replica_groups=mesh['dp'=2,'gx'=4,'gy'=4] {'dp','gx'}, dimensions={0}, use_global_device_ids=true | all-gather | bytes 921600 | tf_op jit(solution)/shard_map/all_gather | solution.py:121
  57.5 36.6 %all_gather.85 = bf16[1280,320]{1,0:T(8,128)(2,1)S(1)} all-gather(bf16[160,320]{1,0:T(8,128)(2,1)S(1)} %copy-done.108), channel_id=1, replica_groups=mesh['dp'=2,'gx'=4,'gy'=4] {'dp','gx'}, dimensions={0}, use_global_device_ids=true | all-gather | bytes 921600 | tf_op jit(solution)/shard_map/all_gather | solution.py:122
  108.2 42.6 %all_gather.87 = bf16[1280,320]{1,0:T(8,128)(2,1)} all-gather(bf16[160,320]{1,0:T(8,128)(2,1)} %param.27), channel_id=1, replica_groups=mesh['dp'=2,'gx'=4,'gy'=4] {'dp','gx'}, dimensions={0}, use_global_device_ids=true | all-gather | bytes 921600 | tf_op jit(solution)/shard_map/all_gather | solution.py:120
  154.0 40.2 %all_gather.90 = bf16[1280,320]{1,0:T(8,128)(2,1)} all-gather(bf16[160,320]{1,0:T(8,128)(2,1)} %param.33), channel_id=1, replica_groups=mesh['dp'=2,'gx'=4,'gy'=4] {'dp','gx'}, dimensions={0}, use_global_device_ids=true | all-gather | bytes 921600 | tf_op jit(solution)/shard_map/all_gather | solution.py:123
  203.9 9.1 fusion.289
  213.0 8.2 fusion
  221.3 8.0 fusion.178
  234.3 9.6 fusion.291
  243.9 8.2 fusion.2
  252.1 8.0 fusion.172
  266.0 9.5 fusion.290
  275.6 8.1 fusion.1
  283.7 15.2 all-gather.38.cloned.1.call-done
  298.9 7.9 fusion.175
  309.8 25.1 %reduce-scatter.27.cloned.1.call-done = f32[128,1,1280]{2,0,1:T(8,128)} async-done(((f32[512,1,1280]{2,0,1:T(8,128)}), f32[128,1,1280]{2,0,1:T(8,128)}) %reduce-scatter.27.cloned.1.call-update) | async-done | bytes 655376 | tf_op jit(solution)/shard_map/reduce_scatter | solution.py:170
  334.9 37.1 %reduce-scatter.35.cloned.1.call-done = f32[128,1,1280]{2,0,1:T(8,128)} async-done(((f32[512,1,1280]{2,0,1:T(8,128)}), f32[128,1,1280]{2,0,1:T(8,128)}) %reduce-scatter.35.cloned.1.call-update) | async-done | bytes 655376 | tf_op jit(solution)/shard_map/reduce_scatter | solution.py:170
  372.0 36.9 %reduce-scatter.31.cloned.1.call-done = f32[128,1,1280]{2,0,1:T(8,128)} async-done(((f32[512,1,1280]{2,0,1:T(8,128)}), f32[128,1,1280]{2,0,1:T(8,128)}) %reduce-scatter.31.cloned.1.call-update) | async-done | bytes 655376 | tf_op jit(solution)/shard_map/reduce_scatter | solution.py:170
  418.3 12.6 all-gather.30.cloned.1.call-done
  430.9 5.7 convolution_add_fusion.12
  436.6 13.8 all-gather.58.cloned.1.call-done
  450.4 63.4 %all-gather.34.cloned.1.call-done = bf16[1280,1280]{1,0:T(8,128)(2,1)} async-done(((bf16[160,1280]{1,0:T(8,128)(2,1)}), bf16[1280,1280]{1,0:T(8,128)(2,1)}) %all-gather.34.cloned.1.call-update) | async-done | bytes 3276816 | tf_op jit(solution)/shard_map/all_gather | solution.py:125
  513.8 6.2 convert_reduce_fusion.2
  524.6 8.1 all-gather.50.cloned.1.call-done
  532.7 5.7 convolution_add_fusion.10
  538.4 14.0 all-gather.62.cloned.1.call-done
  552.4 6.2 convert_reduce_fusion
  563.4 9.0 all-gather.42.cloned.1.call-done
  572.4 5.7 convolution_add_fusion.11
  578.2 13.8 all-gather.60.cloned.1.call-done
  591.9 6.2 convert_reduce_fusion.1
  602.8 6.2 fusion.41
  609.0 6.2 fusion.42
  615.3 6.0 fusion.40
  621.3 7.4 reduce-scatter.39.cloned.1.call-done
  628.8 37.0 %reduce-scatter.55.cloned.1.call-done = f32[128,1,1280]{2,0,1:T(8,128)} async-done(((f32[512,1,1280]{2,0,1:T(8,128)}), f32[128,1,1280]{2,0,1:T(8,128)}) %reduce-scatter.55.cloned.1.call-update) | async-done | bytes 655376 | tf_op jit(solution)/shard_map/reduce_scatter | solution.py:213
  665.7 36.8 %reduce-scatter.47.cloned.1.call-done = f32[128,1,1280]{2,0,1:T(8,128)} async-done(((f32[512,1,1280]{2,0,1:T(8,128)}), f32[128,1,1280]{2,0,1:T(8,128)}) %reduce-scatter.47.cloned.1.call-update) | async-done | bytes 655376 | tf_op jit(solution)/shard_map/reduce_scatter | solution.py:213
  705.4 26.1 %reduce-scatter.33.cloned.1.call-done = bf16[128,1,1280]{2,0,1:T(8,128)(2,1)} async-done(((bf16[512,1,1280]{2,0,1:T(8,128)(2,1)}), bf16[128,1,1280]{2,0,1:T(8,128)(2,1)}) %reduce-scatter.33.cloned.1.call-update) | async-done | bytes 327696 | tf_op jit(solution)/shard_map/reduce_scatter | solution.py:188
  735.2 25.7 %reduce-scatter.37.cloned.1.call-done = bf16[128,1,1280]{2,0,1:T(8,128)(2,1)} async-done(((bf16[512,1,1280]{2,0,1:T(8,128)(2,1)}), bf16[128,1,1280]{2,0,1:T(8,128)(2,1)}) %reduce-scatter.37.cloned.1.call-update) | async-done | bytes 327696 | tf_op jit(solution)/shard_map/reduce_scatter | solution.py:188
  760.8 28.9 %reduce-scatter.29.cloned.1.call-done = bf16[128,1,1280]{2,0,1:T(8,128)(2,1)} async-done(((bf16[512,1,1280]{2,0,1:T(8,128)(2,1)}), bf16[128,1,1280]{2,0,1:T(8,128)(2,1)}) %reduce-scatter.29.cloned.1.call-update) | async-done | bytes 327696 | tf_op jit(solution)/shard_map/reduce_scatter | solution.py:188
  797.4 14.0 multiply_reduce_fusion.1
  814.4 7.9 multiply_convert_fusion.1
  829.7 10.0 fusion.34
  843.3 13.8 multiply_reduce_fusion.2
  860.0 7.8 multiply_convert_fusion.2
  875.2 10.1 fusion.31
  888.8 13.8 multiply_reduce_fusion
  905.7 7.8 multiply_convert_fusion
  920.9 10.1 fusion.37
  935.0 6.1 broadcast_multiply_fusion.1
  953.4 6.5 broadcast_multiply_fusion.2
  963.2 31.7 %reduce-scatter.41.cloned.1.call-done = f32[512,1,4,80]{0,3,2,1:T(8,128)} async-done(((f32[2048,1,4,80]{0,3,2,1:T(8,128)}), f32[512,1,4,80]{0,3,2,1:T(8,128)}) %reduce-scatter.41.cloned.1.call-update) | async-done | bytes 655376 | tf_op jit(solution)/shard_map/reduce_scatter | solution.py:254
  997.0 52.1 %reduce-scatter.43.cloned.1.call-done = f32[512,1,4,80]{0,3,2,1:T(8,128)} async-done(((f32[2048,1,4,80]{0,3,2,1:T(8,128)}), f32[512,1,4,80]{0,3,2,1:T(8,128)}) %reduce-scatter.43.cloned.1.call-update) | async-done | bytes 655376 | tf_op jit(solution)/shard_map/reduce_scatter | solution.py:255
  1055.0 7.0 broadcast_multiply_fusion
  1065.4 37.7 %reduce-scatter.57.cloned.1.call-done = f32[512,1,4,80]{0,3,2,1:T(8,128)} async-done(((f32[2048,1,4,80]{0,3,2,1:T(8,128)}), f32[512,1,4,80]{0,3,2,1:T(8,128)}) %reduce-scatter.57.cloned.1.call-update) | async-done | bytes 655376 | tf_op jit(solution)/shard_map/reduce_scatter | solution.py:254
  1105.1 52.1 %reduce-scatter.59.cloned.1.call-done = f32[512,1,4,80]{0,3,2,1:T(8,128)} async-done(((f32[2048,1,4,80]{0,3,2,1:T(8,128)}), f32[512,1,4,80]{0,3,2,1:T(8,128)}) %reduce-scatter.59.cloned.1.call-update) | async-done | bytes 655376 | tf_op jit(solution)/shard_map/reduce_scatter | solution.py:255
  1181.6 4.7 fusion.6
  1186.4 8.2 copy.41
  1215.1 28.4 %reduce-scatter.61.cloned.1.call-done = bf16[128,1,1280]{2,0,1:T(8,128)(2,1)} async-done(((bf16[512,1,1280]{2,0,1:T(8,128)(2,1)}), bf16[128,1,1280]{2,0,1:T(8,128)(2,1)}) %reduce-scatter.61.cloned.1.call-update) | async-done | bytes 327696 | tf_op jit(solution)/shard_map/reduce_scatter | solution.py:286
  1262.2 53.0 %reduce-scatter.69.cloned.1.call-done = f32[160,320]{1,0:T(8,128)} async-done(((f32[1280,320]{1,0:T(8,128)}), f32[160,320]{1,0:T(8,128)}) %reduce-scatter.69.cloned.1.call-update) | async-done | bytes 204816 | tf_op jit(solution)/shard_map/reduce_scatter | solution.py:300
  1315.2 70.8 %reduce-scatter.63.cloned.1.call-done = f32[160,320]{1,0:T(8,128)} async-done(((f32[1280,320]{1,0:T(8,128)}), f32[160,320]{1,0:T(8,128)}) %reduce-scatter.63.cloned.1.call-update) | async-done | bytes 204816 | tf_op jit(solution)/shard_map/reduce_scatter | solution.py:297
  1386.0 124.7 %reduce-scatter.73.cloned.1.call-done = f32[160,1280]{1,0:T(8,128)} async-done(((f32[1280,1280]{1,0:T(8,128)}), f32[160,1280]{1,0:T(8,128)}) %reduce-scatter.73.cloned.1.call-update) | async-done | bytes 819216
  1510.7 125.2 %reduce-scatter.71.cloned.1.call-done = f32[160,1280]{1,0:T(8,128)} async-done(((f32[1280,1280]{1,0:T(8,128)}), f32[160,1280]{1,0:T(8,128)}) %reduce-scatter.71.cloned.1.call-update) | async-done | bytes 819216 | tf_op jit(solution)/shard_map/reduce_scatter | solution.py:301
  1635.9 70.9 %reduce-scatter.67.cloned.1.call-done = f32[160,320]{1,0:T(8,128)} async-done(((f32[1280,320]{1,0:T(8,128)}), f32[160,320]{1,0:T(8,128)}) %reduce-scatter.67.cloned.1.call-update) | async-done | bytes 204816 | tf_op jit(solution)/shard_map/reduce_scatter | solution.py:299
  1706.8 70.3 %reduce-scatter.65.cloned.1.call-done = f32[160,320]{1,0:T(8,128)} async-done(((f32[1280,320]{1,0:T(8,128)}), f32[160,320]{1,0:T(8,128)}) %reduce-scatter.65.cloned.1.call-update) | async-done | bytes 204816 | tf_op jit(solution)/shard_map/reduce_scatter | solution.py:298
  (653 shorter events, 236.5 us)
Async XLA Ops:
  8.0 45.2 %all-gather.24.cloned.1.call-start = ((), (), s32[]{:S(2)}) async-start(), calls=%async_computation.24 | async-start | bytes 1638400 | tf_op jit(solution)/shard_map/all_gather | solution.py:130
  13.3 84.6 %all-gather.44.cloned.1.call-start = ((), (), s32[]{:S(2)}) async-start(), calls=%async_computation.38 | async-start | bytes 1638400 | tf_op jit(solution)/shard_map/all_gather | solution.py:130
  14.1 136.8 %all-gather.36.cloned.1.call-start = ((), (), s32[]{:S(2)}) async-start(), calls=%async_computation.32 | async-start | bytes 1638400 | tf_op jit(solution)/shard_map/all_gather | solution.py:130
  14.8 189.1 %all-gather.28.cloned.1.call-start = ((), (), s32[]{:S(2)}) async-start(), calls=%async_computation.26 | async-start | bytes 1638400 | tf_op jit(solution)/shard_map/all_gather | solution.py:148
  15.8 82.1 %copy-start.161 = (f32[320]{0:T(512)}, f32[320]{0:T(512)S(1)}, u32[]{:S(2)}) copy-start(f32[320]{0:T(512)S(1)} %dynamic_slice.34) | copy-start | bytes 3844
  15.9 81.3 %copy-start.93 = (f32[512,1,20]{0,2,1:T(8,128)}, f32[512,1,20]{0,2,1:T(8,128)S(1)}, u32[]{:S(2)}) copy-start(f32[512,1,20]{0,2,1:T(8,128)S(1)} %get-tuple-element.221) | copy-start | bytes 122884
  15.9 81.3 %copy-start.95 = (f32[512,1,20]{0,2,1:T(8,128)}, f32[512,1,20]{0,2,1:T(8,128)S(1)}, u32[]{:S(2)}) copy-start(f32[512,1,20]{0,2,1:T(8,128)S(1)} %get-tuple-element.222) | copy-start | bytes 122884
  15.9 91.7 %copy-start.97 = (f32[512,1,20]{0,2,1:T(8,128)}, f32[512,1,20]{0,2,1:T(8,128)S(1)}, u32[]{:S(2)}) copy-start(f32[512,1,20]{0,2,1:T(8,128)S(1)} %get-tuple-element.219) | copy-start | bytes 122884
  15.9 91.7 %copy-start.99 = (f32[512,1,20]{0,2,1:T(8,128)}, f32[512,1,20]{0,2,1:T(8,128)S(1)}, u32[]{:S(2)}) copy-start(f32[512,1,20]{0,2,1:T(8,128)S(1)} %get-tuple-element.220) | copy-start | bytes 122884
  53.3 97.6 %copy-start.5 = (bf16[1280,320]{1,0:T(8,128)(2,1)}, bf16[1280,320]{1,0:T(8,128)(2,1)S(1)}, u32[]{:S(2)}) copy-start(bf16[1280,320]{1,0:T(8,128)(2,1)S(1)} %all_gather.88) | copy-start | bytes 2457604
  56.7 164.6 %all-gather.26.cloned.1.call-start = ((), (), s32[]{:S(2)}) async-start(), calls=%async_computation.25 | async-start | bytes 1638400 | tf_op jit(solution)/shard_map/all_gather | solution.py:149
  57.5 45.5 %copy-start.162 = (f32[320]{0:T(512)}, f32[320]{0:T(512)S(1)}, u32[]{:S(2)}) copy-start(f32[320]{0:T(512)S(1)} %dynamic_slice.30) | copy-start | bytes 3844
  94.1 106.5 %copy-start.7 = (bf16[1280,320]{1,0:T(8,128)(2,1)}, bf16[1280,320]{1,0:T(8,128)(2,1)S(1)}, u32[]{:S(2)}) copy-start(bf16[1280,320]{1,0:T(8,128)(2,1)S(1)} %all_gather.85) | copy-start | bytes 2457604
  97.2 137.1 %all-gather.48.cloned.1.call-start = ((), (), s32[]{:S(2)}) async-start(), calls=%async_computation.40 | async-start | bytes 1638400 | tf_op jit(solution)/shard_map/all_gather | solution.py:148
  97.9 136.2 %copy-start.58 = (f32[512,80]{0,1:T(8,128)}, f32[512,80]{0,1:T(8,128)S(1)}, u32[]{:S(2)}) copy-start(f32[512,80]{0,1:T(8,128)S(1)} %get-tuple-element.189) | copy-start | bytes 491524
  101.0 151.1 %all-gather.46.cloned.1.call-start = ((), (), s32[]{:S(2)}) async-start(), calls=%async_computation.39 | async-start | bytes 1638400 | tf_op jit(solution)/shard_map/all_gather | solution.py:149
  105.7 160.3 %all-gather.40.cloned.1.call-start = ((), (), s32[]{:S(2)}) async-start(), calls=%async_computation.34 | async-start | bytes 1638400 | tf_op jit(solution)/shard_map/all_gather | solution.py:148
  153.9 45.0 %copy-start.9 = (bf16[1280,320]{1,0:T(8,128)(2,1)S(1)}, bf16[1280,320]{1,0:T(8,128)(2,1)}, u32[]{:S(2)}) copy-start(bf16[1280,320]{1,0:T(8,128)(2,1)} %all_gather.87) | copy-start | bytes 2457604
  153.9 45.0 %copy-start.160 = (f32[320]{0:T(512)S(1)}, f32[320]{0:T(512)}, u32[]{:S(2)}) copy-start(f32[320]{0:T(512)} %dynamic_slice.32) | copy-start | bytes 3844
  154.0 144.9 %all-gather.38.cloned.1.call-start = ((), (), s32[]{:S(2)}) async-start(), calls=%async_computation.33 | async-start | bytes 1638400 | tf_op jit(solution)/shard_map/all_gather | solution.py:149
  154.0 44.9 %copy-start.13 = (bf16[512,1,1280]{2,0,1:T(8,128)(2,1)S(1)}, bf16[512,1,1280]{2,0,1:T(8,128)(2,1)}, u32[]{:S(2)}) copy-start(bf16[512,1,1280]{2,0,1:T(8,128)(2,1)} %all-gather.24.cloned.1.call-done) | copy-start | bytes 3932164
  202.0 132.9 %reduce-scatter.27.cloned.1.call-start = ((), (), s32[]{:S(2)}) async-start(), calls=%async_computation.27 | async-start | bytes 3276800 | tf_op jit(solution)/shard_map/reduce_scatter | solution.py:170
  231.7 140.3 %reduce-scatter.35.cloned.1.call-start = ((), (), s32[]{:S(2)}) async-start(), calls=%async_computation.41 | async-start | bytes 3276800 | tf_op jit(solution)/shard_map/reduce_scatter | solution.py:170
  263.3 145.7 %reduce-scatter.31.cloned.1.call-start = ((), (), s32[]{:S(2)}) async-start(), calls=%async_computation.35 | async-start | bytes 3276800 | tf_op jit(solution)/shard_map/reduce_scatter | solution.py:170
  306.8 102.1 %copy-start.140 = (f32[1280]{0:T(1024)S(1)}, f32[1280]{0:T(1024)}, u32[]{:S(2)}) copy-start(f32[1280]{0:T(1024)} %param.34) | copy-start | bytes 15364
  309.2 109.1 %all-gather.32.cloned.1.call-start = ((), (), s32[]{:S(2)}) async-start(), calls=%async_computation.29 | async-start | bytes 3686400 | tf_op jit(solution)/shard_map/all_gather | solution.py:124
  309.8 101.7 %copy-start.105 = (f32[1280]{0:T(1024)S(1)}, f32[1280]{0:T(1024)}, u32[]{:S(2)}) copy-start(f32[1280]{0:T(1024)} %param.35) | copy-start | bytes 15364
  309.8 101.7 %copy-start.141 = (f32[1280]{0:T(1024)S(1)}, f32[1280]{0:T(1024)}, u32[]{:S(2)}) copy-start(f32[1280]{0:T(1024)} %param.36) | copy-start | bytes 15364
  309.8 121.1 %all-gather.30.cloned.1.call-start = ((), (), s32[]{:S(2)}) async-start(), calls=%async_computation.28 | async-start | bytes 1638400 | tf_op jit(solution)/shard_map/all_gather | solution.py:180
  412.8 37.6 %all-gather.58.cloned.1.call-start = ((), (), s32[]{:S(2)}) async-start(), calls=%async_computation.59 | async-start | bytes 1638400 | tf_op jit(solution)/shard_map/all_gather | solution.py:201
  413.8 100.0 %all-gather.34.cloned.1.call-start = ((), (), s32[]{:S(2)}) async-start(), calls=%async_computation.30 | async-start | bytes 3686400 | tf_op jit(solution)/shard_map/all_gather | solution.py:125
  414.6 118.1 %all-gather.50.cloned.1.call-start = ((), (), s32[]{:S(2)}) async-start(), calls=%async_computation.42 | async-start | bytes 1638400 | tf_op jit(solution)/shard_map/all_gather | solution.py:180
  415.3 137.0 %all-gather.62.cloned.1.call-start = ((), (), s32[]{:S(2)}) async-start(), calls=%async_computation.61 | async-start | bytes 1638400 | tf_op jit(solution)/shard_map/all_gather | solution.py:201
  416.1 156.4 %all-gather.42.cloned.1.call-start = ((), (), s32[]{:S(2)}) async-start(), calls=%async_computation.36 | async-start | bytes 1638400 | tf_op jit(solution)/shard_map/all_gather | solution.py:180
  416.7 175.3 %all-gather.60.cloned.1.call-start = ((), (), s32[]{:S(2)}) async-start(), calls=%async_computation.60 | async-start | bytes 1638400 | tf_op jit(solution)/shard_map/all_gather | solution.py:201
  417.2 211.5 %reduce-scatter.39.cloned.1.call-start = ((), (), s32[]{:S(2)}) async-start(), calls=%async_computation.44 | async-start | bytes 3276800 | tf_op jit(solution)/shard_map/reduce_scatter | solution.py:213
  524.5 141.2 %reduce-scatter.55.cloned.1.call-start = ((), (), s32[]{:S(2)}) async-start(), calls=%async_computation.54 | async-start | bytes 3276800 | tf_op jit(solution)/shard_map/reduce_scatter | solution.py:213
  563.1 139.4 %reduce-scatter.47.cloned.1.call-start = ((), (), s32[]{:S(2)}) async-start(), calls=%async_computation.49 | async-start | bytes 3276800 | tf_op jit(solution)/shard_map/reduce_scatter | solution.py:213
  602.7 128.7 %reduce-scatter.33.cloned.1.call-start = ((), (), s32[]{:S(2)}) async-start(), calls=%async_computation.37 | async-start | bytes 1638400 | tf_op jit(solution)/shard_map/reduce_scatter | solution.py:188
  609.0 151.9 %reduce-scatter.37.cloned.1.call-start = ((), (), s32[]{:S(2)}) async-start(), calls=%async_computation.43 | async-start | bytes 1638400 | tf_op jit(solution)/shard_map/reduce_scatter | solution.py:188
  615.2 174.6 %reduce-scatter.29.cloned.1.call-start = ((), (), s32[]{:S(2)}) async-start(), calls=%async_computation.31 | async-start | bytes 1638400 | tf_op jit(solution)/shard_map/reduce_scatter | solution.py:188
  621.3 110.2 %copy-start.121 = (f32[1280]{0:T(1024)S(1)}, f32[1280]{0:T(1024)}, u32[]{:S(2)}) copy-start(f32[1280]{0:T(1024)} %param.40) | copy-start | bytes 15364
  621.3 173.4 %all-gather.54.cloned.1.call-start = ((), (), s32[]{:S(2)}) async-start(), calls=%async_computation.50 | async-start | bytes 1638400 | tf_op jit(solution)/shard_map/all_gather | solution.py:226
  734.7 105.8 %all-gather.52.cloned.1.call-start = ((), (), s32[]{:S(2)}) async-start(), calls=%async_computation.45 | async-start | bytes 1638400 | tf_op jit(solution)/shard_map/all_gather | solution.py:226
  735.2 59.5 %copy-start.12 = (bf16[1280,320]{1,0:T(8,128)(2,1)S(1)}, bf16[1280,320]{1,0:T(8,128)(2,1)}, u32[]{:S(2)}) copy-start(bf16[1280,320]{1,0:T(8,128)(2,1)} %all_gather.90) | copy-start | bytes 2457604
  794.0 92.1 %all-gather.56.cloned.1.call-start = ((), (), s32[]{:S(2)}) async-start(), calls=%async_computation.55 | async-start | bytes 1638400 | tf_op jit(solution)/shard_map/all_gather | solution.py:226
  794.6 150.2 %reduce-scatter.49.cloned.1.call-start = ((), (), s32[]{:S(2)}) async-start(), calls=%async_computation.51 | async-start | bytes 3276800 | tf_op jit(solution)/shard_map/reduce_scatter | solution.py:254
  828.7 118.1 %reduce-scatter.51.cloned.1.call-start = ((), (), s32[]{:S(2)}) async-start(), calls=%async_computation.52 | async-start | bytes 3276800 | tf_op jit(solution)/shard_map/reduce_scatter | solution.py:255
  839.8 155.2 %reduce-scatter.41.cloned.1.call-start = ((), (), s32[]{:S(2)}) async-start(), calls=%async_computation.46 | async-start | bytes 3276800 | tf_op jit(solution)/shard_map/reduce_scatter | solution.py:254
  874.3 174.8 %reduce-scatter.43.cloned.1.call-start = ((), (), s32[]{:S(2)}) async-start(), calls=%async_computation.47 | async-start | bytes 3276800 | tf_op jit(solution)/shard_map/reduce_scatter | solution.py:255
  885.4 217.7 %reduce-scatter.57.cloned.1.call-start = ((), (), s32[]{:S(2)}) async-start(), calls=%async_computation.56 | async-start | bytes 3276800 | tf_op jit(solution)/shard_map/reduce_scatter | solution.py:254
  920.0 237.2 %reduce-scatter.59.cloned.1.call-start = ((), (), s32[]{:S(2)}) async-start(), calls=%async_computation.57 | async-start | bytes 3276800 | tf_op jit(solution)/shard_map/reduce_scatter | solution.py:255
  931.1 284.0 %reduce-scatter.53.cloned.1.call-start = ((), (), s32[]{:S(2)}) async-start(), calls=%async_computation.53 | async-start | bytes 1638400 | tf_op jit(solution)/shard_map/reduce_scatter | solution.py:286
  952.9 262.2 %reduce-scatter.45.cloned.1.call-start = ((), (), s32[]{:S(2)}) async-start(), calls=%async_computation.48 | async-start | bytes 1638400 | tf_op jit(solution)/shard_map/reduce_scatter | solution.py:286
  963.2 87.3 %copy-start.64 = (f32[512,80]{0,1:T(8,128)S(1)}, f32[512,80]{0,1:T(8,128)}, u32[]{:S(2)}) copy-start(f32[512,80]{0,1:T(8,128)} %copy-done.63) | copy-start | bytes 491524
  1055.0 188.6 %reduce-scatter.61.cloned.1.call-start = ((), (), s32[]{:S(2)}) async-start(), calls=%async_computation.58 | async-start | bytes 1638400 | tf_op jit(solution)/shard_map/reduce_scatter | solution.py:286
  1065.3 93.3 %copy-start.59 = (f32[512,80]{0,1:T(8,128)S(1)}, f32[512,80]{0,1:T(8,128)}, u32[]{:S(2)}) copy-start(f32[512,80]{0,1:T(8,128)} %copy-done.58) | copy-start | bytes 491524
  1163.2 152.0 %reduce-scatter.69.cloned.1.call-start = ((), (), s32[]{:S(2)}) async-start(), calls=%async_computation.65 | async-start | bytes 2211840 | tf_op jit(solution)/shard_map/reduce_scatter | solution.py:300
  1169.6 216.4 %reduce-scatter.63.cloned.1.call-start = ((), (), s32[]{:S(2)}) async-start(), calls=%async_computation.62 | async-start | bytes 2211840 | tf_op jit(solution)/shard_map/reduce_scatter | solution.py:297
  1175.1 335.5 %reduce-scatter.73.cloned.1.call-start = ((), (), s32[]{:S(2)}) async-start(), calls=%async_computation.67 | async-start | bytes 7372800
  1194.6 441.3 %reduce-scatter.71.cloned.1.call-start = ((), (), s32[]{:S(2)}) async-start(), calls=%async_computation.66 | async-start | bytes 7372800 | tf_op jit(solution)/shard_map/reduce_scatter | solution.py:301
  1205.6 430.2 %all-reduce.3.cloned.1.call-start = ((), (), s32[]{:S(2)}) async-start(), calls=%async_computation.68 | async-start | bytes 188416 | tf_op jit(solution)/shard_map/psum | solution.py:317
  1247.0 459.8 %reduce-scatter.67.cloned.1.call-start = ((), (), s32[]{:S(2)}) async-start(), calls=%async_computation.64 | async-start | bytes 2211840 | tf_op jit(solution)/shard_map/reduce_scatter | solution.py:299
  1251.2 525.9 %reduce-scatter.65.cloned.1.call-start = ((), (), s32[]{:S(2)}) async-start(), calls=%async_computation.63 | async-start | bytes 2211840 | tf_op jit(solution)/shard_map/reduce_scatter | solution.py:298
  (165 other events, 1567.3 us)
Sparse Core Ops, SparseCore 0:
  13.4 20.8 all-gather.23
  36.5 18.1 all-gather.43
  56.8 18.1 all-gather.35
  76.4 38.0 all-gather.27
  115.9 43.1 all-gather.25
  160.6 37.9 all-gather.47
  200.2 32.1 all-gather.45
  233.9 31.7 all-gather.39
  267.3 31.5 all-gather.37
  301.3 33.6 reduce-scatter.26
  337.5 34.4 reduce-scatter.34
  374.4 34.4 reduce-scatter.30
  734.8 18.1 all-gather.53
  794.1 18.1 all-gather.51
  814.3 18.1 all-gather.55
  834.7 52.2 reduce-scatter.48
  889.1 51.7 reduce-scatter.50
  943.1 51.7 reduce-scatter.40
  997.2 51.7 reduce-scatter.42
  1051.2 51.7 reduce-scatter.56
  1105.4 51.7 reduce-scatter.58
  1159.7 25.9 reduce-scatter.52
  1188.3 26.4 reduce-scatter.44
  1217.1 26.3 reduce-scatter.60
  1247.6 67.5 reduce-scatter.68
  1319.1 66.8 reduce-scatter.62
  1390.0 120.6 reduce-scatter.72
  1514.9 120.9 reduce-scatter.70
  1639.9 66.8 reduce-scatter.66
  1710.7 66.3 reduce-scatter.64
Sparse Core Ops, SparseCore 1:
  311.8 60.4 all-gather.31
  412.8 18.0 all-gather.29
  432.3 18.0 all-gather.57
  452.5 61.3 all-gather.33
  516.0 16.7 all-gather.49
  534.3 18.0 all-gather.61
  554.4 18.0 all-gather.41
  573.9 18.0 all-gather.59
  594.3 34.4 reduce-scatter.38
  631.3 34.4 reduce-scatter.54
  668.1 34.3 reduce-scatter.46
  705.1 26.3 reduce-scatter.32
  734.4 26.3 reduce-scatter.36
  763.4 26.3 reduce-scatter.28
  1247.1 138.3 all-reduce.2
where the time goes:
time: 1810 us; the launch traced here: 1800 us
  waiting for transfers between devices  1130 us (62%)
  matrix products  311 us (17%)
  blocking collectives  156 us (9%)
  other arithmetic  111 us (6%)
  local copies, waits for them, and re-layouts  61.2 us (3%)
  between operations  19.2 us (1%)
    unnamed x46, waiting for transfers between devices  131 us
    reduce_scatter x1, waiting for transfers between devices, per_device(): lax.psum_scatter(grad_up, ('dp', 'gx'), scatter_dimension=0, tiled=True)  125 us
    reduce_scatter x3, waiting for transfers between devices, per_device(): lax.psum_scatter(value_part, 'gx', scatter_dimension=0, tiled=True)  104 us
    reduce_scatter x3, waiting for transfers between devices, per_device(): lax.psum_scatter(jnp.einsum('srh,oh->sro', mixture, full_out, preferred_e...  99.1 us
    reduce_scatter x3, waiting for transfers between devices, per_device(): lax.psum_scatter(jnp.einsum('srf,df->srd', hidden_grad, full_up, preferre...  81.2 us
    reduce_scatter x3, waiting for transfers between devices, per_device(): lax.psum_scatter(jnp.einsum('srf,of->sro', active, full_down, preferred_e...  80.7 us
    reduce_scatter x1, waiting for transfers between devices, per_device(): lax.psum_scatter(grad_value, ('dp', 'gx'), scatter_dimension=0, tiled=True)  70.9 us
    reduce_scatter x1, waiting for transfers between devices, per_device(): lax.psum_scatter(grad_query, ('dp', 'gx'), scatter_dimension=0, tiled=True)  70.8 us
  transfers between devices with their start and end apart: 45, of which 28 were waited for; matrix products, arithmetic and copies ran while one was open for 24% of the time, Pallas kernels for 0%

commit v1 on v0

v1 whole, which is shorter than its diff:
```python
import functools

import jax
import jax.numpy as jnp
from jax import lax
from jax.experimental import pallas as pl
from jax.experimental.pallas import tpu as pltpu
from jax.sharding import PartitionSpec as P

HEAD_DIM = 80
HALF = HEAD_DIM // 2
PACK = 256
EPSILON = 1e-06
MAP = (0, 2, 1, 3)
BLK = 256
LOG2E = 1.4426950408889634
SCALE = HEAD_DIM ** (-0.5)
F32 = jnp.float32
BF16 = jnp.bfloat16
NT = (((1,), (1,)), ((), ()))


def dot(a, b):
    return jnp.dot(a, b, preferred_element_type=F32)


def dot_nt(a, b):
    return lax.dot_general(a, b, NT, preferred_element_type=F32)


def turn(v):
    return jnp.transpose(v.astype(F32))


VM = pl.BlockSpec(memory_space=pltpu.VMEM)
SM = pl.BlockSpec(memory_space=pltpu.SMEM)


def call(body, specs, outs, scratch, flops, nbytes, name, trans=0):
    return pl.pallas_call(
        body,
        in_specs=specs,
        out_specs=[VM] * len(outs),
        out_shape=[jax.ShapeDtypeStruct(s, d) for s, d in outs],
        scratch_shapes=[pltpu.VMEM(s, d) for s, d in scratch],
        cost_estimate=pl.CostEstimate(flops=flops, bytes_accessed=nbytes, transcendentals=trans),
        name=name,
    )


def head_of(p, dup):
    return p if dup == 1 else lax.div(p, dup)


def place_rows(s_ref, pieces, out, rows):
    for p in range(4):
        c = lax.bitwise_xor(s_ref[1], MAP[p])
        out[pl.ds(pl.multiple_of(c * rows, rows), rows), :] = pieces[p // 2][
            (p % 2) * rows : (p % 2 + 1) * rows, :
        ]


def split_rows(s_ref, src, keep, send, rows):
    for p in range(4):
        c = lax.bitwise_xor(s_ref[1], MAP[p])
        dst = (keep, send)[p // 2]
        dst[(p % 2) * rows : (p % 2 + 1) * rows, :] = src[
            pl.ds(pl.multiple_of(c * rows, rows), rows), :
        ]


def qkv_body(gx, dup, rows, s_ref, xa, xb, w, b, cos, sin, *rest):
    outs, xn = rest[:gx], rest[gx]
    place_rows(s_ref, (xa, xb), xn, rows)
    for r in range(gx):
        hh = head_of(lax.rem(s_ref[0] + r, gx), dup)
        cols = pl.ds(pl.multiple_of(hh * PACK, PACK), PACK)
        t = turn(dot(xn[...], w[:, cols]) + b[:, cols])
        c, s = cos[...], sin[...]
        for k in (0, 1):
            lo = t[k * HEAD_DIM : k * HEAD_DIM + HALF]
            hi = t[k * HEAD_DIM + HALF : (k + 1) * HEAD_DIM]
            both = jnp.concatenate([lo * c - hi * s, hi * c + lo * s], axis=0)
            outs[r][k * HEAD_DIM : (k + 1) * HEAD_DIM, :] = both.astype(BF16)
        outs[r][2 * HEAD_DIM : 3 * HEAD_DIM, :] = t[2 * HEAD_DIM : 3 * HEAD_DIM].astype(BF16)


def attend_body(gx, slots, s_ref, lim_ref, *rest):
    blocks = rest[:gx]
    idr, idc = rest[gx : gx + 2]
    outs = rest[gx + 2 : 2 * gx + 2]
    full, lse, mix, keys = rest[2 * gx + 2 :]
    qr = slots // gx
    nb = slots // BLK
    for r in range(gx):
        p = lax.rem(s_ref[0] + (gx - r), gx)
        full[:, pl.ds(pl.multiple_of(p * qr, qr), qr)] = blocks[r][...]
    for c in range(nb):
        keys[c * BLK : (c + 1) * BLK, :] = turn(
            full[HEAD_DIM : 2 * HEAD_DIM, c * BLK : (c + 1) * BLK]
        ).astype(BF16)

    def one(qb, carry):
        at = pl.ds(pl.multiple_of(qb * BLK, BLK), BLK)
        q = full[0:HEAD_DIM, at]
        qid = idr[:, at]

        def inner(kb, state):
            high, total, acc = state
            kat = pl.ds(pl.multiple_of(kb * BLK, BLK), BLK)
            s = dot(keys[kat, :], q)
            kid = idc[kat, :]
            kid = jnp.concatenate([kid] * (BLK // 128), axis=1)
            s = jnp.where(kid == qid, s * (SCALE * LOG2E), -1e30)
            top = jnp.maximum(high, jnp.max(s, axis=0, keepdims=True))
            e = jnp.exp2(s - top)
            fade = jnp.exp2(high - top)
            total = fade * total + jnp.sum(e, axis=0, keepdims=True)
            acc = fade * acc + dot(full[2 * HEAD_DIM : 3 * HEAD_DIM, kat], e.astype(BF16))
            return top, total, acc

        high, total, acc = lax.fori_loop(
            lim_ref[0, qb],
            lim_ref[1, qb] + 1,
            inner,
            (
                jnp.full((1, BLK), -1e30, F32),
                jnp.zeros((1, BLK), F32),
                jnp.zeros((HEAD_DIM, BLK), F32),
            ),
        )
        mix[:, at] = (acc / total).astype(BF16)
        lse[:, at] = high + jnp.log2(total)
        return carry

    lax.fori_loop(0, nb, one, 0)
    for r in range(gx):
        p = lax.rem(s_ref[0] + r, gx)
        outs[r][...] = mix[:, pl.ds(pl.multiple_of(p * qr, qr), qr)]


def project_body(gx, dup, rows, s_ref, *rest):
    blocks, wo = rest[:gx], rest[gx]
    mix, keep, send, flat, full = rest[gx + 1 :]
    for r in range(gx):
        hh = head_of(lax.rem(s_ref[0] + (gx - r), gx), dup)
        flat[pl.ds(pl.multiple_of(hh * HEAD_DIM, 16), HEAD_DIM), :] = blocks[r][...]
    mix[...] = turn(flat[...]).astype(BF16)
    full[...] = dot_nt(mix[...], wo[...]).astype(BF16)
    split_rows(s_ref, full, keep, send, rows)


def mlp_body(xa, xb, ca, cb, up, down, bias, act, hg, ra, rb, na, nb_, total):
    width = up.shape[1]
    depth = up.shape[0]
    n = xa.shape[0]
    total[...] = jnp.zeros_like(total)
    for h, (x, c, res, ng) in enumerate(((xb, cb, rb, nb_), (xa, ca, ra, na))):
        base = (1 - h) * n

        def first(t, carry):
            at = pl.ds(pl.multiple_of(t * 256, 256), 256)
            hidden = dot(x[...], up[:, at]) + bias[:, at]
            s = 1.0 / (1.0 + jnp.exp2(hidden * (-1.702 * LOG2E)))
            act[base : base + n, at] = (hidden * s).astype(BF16)
            g = dot(c[...], down[:, at]) * (s + 1.702 * hidden * s * (1.0 - s))
            g = g.astype(BF16)
            hg[base : base + n, at] = g
            total[:, at] = total[:, at] + jnp.sum(g.astype(F32), axis=0, keepdims=True)
            return carry

        lax.fori_loop(0, width // 256, first, 0)

        def second(t, carry):
            at = pl.ds(pl.multiple_of(t * 256, 256), 256)
            res[:, at] = dot_nt(act[base : base + n, :], down[at, :]).astype(BF16)
            ng[:, at] = dot_nt(hg[base : base + n, :], up[at, :]).astype(BF16)
            return carry

        lax.fori_loop(0, depth // 256, second, 0)


def mix_grad_body(gx, dup, rows, s_ref, ba, bb, wo, *rest):
    outs, brn, flat = rest[:gx], rest[gx], rest[gx + 1]
    place_rows(s_ref, (ba, bb), brn, rows)
    flat[...] = turn(dot(brn[...], wo[...])).astype(BF16)
    for r in range(gx):
        hh = head_of(lax.rem(s_ref[0] + r, gx), dup)
        outs[r][...] = flat[pl.ds(pl.multiple_of(hh * HEAD_DIM, 16), HEAD_DIM), :]


def attend_back_body(gx, slots, s_ref, lim_ref, *rest):
    full, lse, idr, idc, cos, sin = rest[:6]
    blocks = rest[6 : 6 + gx]
    outs = rest[6 + gx : 6 + 2 * gx]
    gt, kn, vn, qn, gn, es, gs, dk, dv, done = rest[6 + 2 * gx :]
    qr = slots // gx
    nb = slots // BLK
    for r in range(gx):
        p = lax.rem(s_ref[0] + (gx - r), gx)
        gt[:, pl.ds(pl.multiple_of(p * qr, qr), qr)] = blocks[r][...]
    for c in range(nb):
        at = slice(c * BLK, (c + 1) * BLK)
        qn[at, :] = turn(full[0:HEAD_DIM, at]).astype(BF16)
        kn[at, :] = turn(full[HEAD_DIM : 2 * HEAD_DIM, at]).astype(BF16)
        vn[at, :] = turn(full[2 * HEAD_DIM : 3 * HEAD_DIM, at]).astype(BF16)
        gn[at, :] = turn(gt[:, at]).astype(BF16)
    dk[...] = jnp.zeros_like(dk)
    dv[...] = jnp.zeros_like(dv)

    def one(qb, carry):
        at = pl.ds(pl.multiple_of(qb * BLK, BLK), BLK)
        first, past = lim_ref[0, qb], lim_ref[1, qb] + 1

        def scores(kb, delta):
            kat = pl.ds(pl.multiple_of(kb * BLK, BLK), BLK)
            s = dot(kn[kat, :], full[0:HEAD_DIM, at])
            kid = idc[kat, :]
            kid = jnp.concatenate([kid] * (BLK // 128), axis=1)
            e = jnp.where(
                kid == idr[:, at], jnp.exp2(s * (SCALE * LOG2E) - lse[:, at]), 0.0
            )
            g = dot(vn[kat, :], gt[:, at])
            es[kat, :] = e
            gs[kat, :] = g
            return delta + jnp.sum(e * g, axis=0, keepdims=True)

        delta = lax.fori_loop(first, past, scores, jnp.zeros((1, BLK), F32))

        def grads(kb, dq):
            kat = pl.ds(pl.multiple_of(kb * BLK, BLK), BLK)
            e = es[kat, :]
            ds = (e * (gs[kat, :] - delta)).astype(BF16)
            dv[kat, :] += dot(e.astype(BF16), gn[at, :])
            dk[kat, :] += dot(ds, qn[at, :])
            return dq + dot(full[HEAD_DIM : 2 * HEAD_DIM, kat], ds)

        dq = lax.fori_loop(first, past, grads, jnp.zeros((HEAD_DIM, BLK), F32)) * SCALE
        c, s = cos[:, at], sin[:, at]
        lo, hi = dq[:HALF], dq[HALF:]
        done[0:HEAD_DIM, at] = jnp.concatenate(
            [lo * c + hi * s, hi * c - lo * s], axis=0
        ).astype(BF16)
        return carry

    lax.fori_loop(0, nb, one, 0)

    def finish(kb, carry):
        at = pl.ds(pl.multiple_of(kb * BLK, BLK), BLK)
        c, s = cos[:, at], sin[:, at]
        back = turn(dk[at, :]) * SCALE
        lo, hi = back[:HALF], back[HALF:]
        done[HEAD_DIM : 2 * HEAD_DIM, at] = jnp.concatenate(
            [lo * c + hi * s, hi * c - lo * s], axis=0
        ).astype(BF16)
        done[2 * HEAD_DIM : 3 * HEAD_DIM, at] = turn(dv[at, :]).astype(BF16)
        return carry

    lax.fori_loop(0, nb, finish, 0)
    for r in range(gx):
        p = lax.rem(s_ref[0] + r, gx)
        outs[r][...] = done[:, pl.ds(pl.multiple_of(p * qr, qr), qr)]


def qkv_back_body(gx, dup, rows, s_ref, *rest):
    blocks, w = rest[:gx], rest[gx]
    d, keep, send, total, full = rest[gx + 1 :]
    for r in range(gx):
        hh = head_of(lax.rem(s_ref[0] + (gx - r), gx), dup)
        t = blocks[r][...].astype(F32)
        t = jnp.concatenate([t, jnp.zeros((PACK - 3 * HEAD_DIM, t.shape[1]), F32)], axis=0)
        d[:, pl.ds(pl.multiple_of(hh * PACK, PACK), PACK)] = jnp.transpose(t).astype(BF16)
    total[...] = jnp.sum(d[...].astype(F32), axis=0, keepdims=True)

    def step(t, carry):
        at = pl.ds(pl.multiple_of(t * 256, 256), 256)
        full[:, at] = dot_nt(d[...], w[at, :]).astype(BF16)
        return carry

    lax.fori_loop(0, w.shape[0] // 256, step, 0)
    split_rows(s_ref, full, keep, send, rows)


def weight_grad_body(n, *rest):
    left, right, out = rest[:n], rest[n : 2 * n], rest[2 * n]

    def step(t, carry):
        at = pl.ds(pl.multiple_of(t * 256, 256), 256)
        acc = None
        for a, b in zip(left, right):
            part = lax.dot_general(
                a[:, at], b[...], (((0,), (0,)), ((), ())), preferred_element_type=F32
            )
            acc = part if acc is None else acc + part
        out[at, :] = acc.astype(BF16)
        return carry

    lax.fori_loop(0, out.shape[0] // 256, step, 0)


def weight_grad(left, right, name):
    d1, d2 = left[0].shape[1], right[0].shape[1]
    k = sum(a.shape[0] for a in left)
    n = len(left)
    return call(
        functools.partial(weight_grad_body, n),
        [VM] * (2 * n),
        [((d1, d2), BF16)],
        [],
        2 * k * d1 * d2,
        2 * (k * (d1 + d2) + d1 * d2),
        name,
    )(*left, *right)[0]


def layer_norm(values, norm_gain, norm_shift):
    center = values - jnp.mean(values, axis=-1, keepdims=True)
    factor = lax.rsqrt(jnp.mean(center * center, axis=-1, keepdims=True) + EPSILON)
    normal = center * factor
    return (normal * norm_gain + norm_shift, normal, factor)


def norm_back(upstream, normal, factor, norm_gain):
    shaped = upstream * norm_gain
    first_mean = jnp.mean(shaped, axis=-1, keepdims=True)
    second_mean = jnp.mean(shaped * normal, axis=-1, keepdims=True)
    return factor * (shaped - first_mean - normal * second_mean)


def per_device(
    block_input,
    picture,
    position,
    patch_mask,
    gain_attn,
    shift_attn,
    w_query,
    b_query,
    w_key,
    b_key,
    w_value,
    b_value,
    w_out,
    b_out,
    gain_mlp,
    shift_mlp,
    w_up,
    b_up,
    w_down,
    b_down,
    out_grad,
):
    gx = lax.axis_size("gx")
    column = lax.axis_index("gy")
    segment = lax.axis_index("gx")
    micros = block_input.shape[0]
    rows = block_input.shape[2]
    width = block_input.shape[3]
    slots = picture.shape[2]
    qr = 4 * rows
    head_cols = w_query.shape[1]
    hidden_cols = w_up.shape[1]
    heads = head_cols // HEAD_DIM
    dup = gx // heads
    assert lax.axis_size("gy") == 4 and dup * heads == gx and slots == qr * gx
    shard_rows = w_query.shape[0]
    head_start = column * head_cols
    up_start = column * hidden_cols
    where = jnp.stack([segment, column]).astype(jnp.int32)
    x_pairs = [(d, d ^ 2) for d in range(4)]
    core_pairs = [(d, d ^ 1) for d in range(4)]
    spins = [[(d, (d + r) % gx) for d in range(gx)] for r in range(gx)]
    over = ("dp", "gx")

    def pack(q, k, v):
        n = q.shape[0]
        parts = [t.reshape(n, heads, HEAD_DIM) for t in (q, k, v)]
        parts.append(jnp.zeros((n, heads, PACK - 3 * HEAD_DIM), q.dtype))
        return jnp.concatenate(parts, axis=2).reshape(n, heads * PACK)

    def unpack(t):
        n = t.shape[0]
        t = t.reshape(n, heads, PACK)
        return [
            t[:, :, k * HEAD_DIM : (k + 1) * HEAD_DIM].reshape(n, head_cols) for k in range(3)
        ]

    full_qkv = lax.all_gather(pack(w_query, w_key, w_value), over, axis=0, tiled=True)
    full_out = lax.all_gather(w_out, over, axis=0, tiled=True)
    full_up = lax.all_gather(w_up, over, axis=0, tiled=True)
    full_down = lax.all_gather(w_down, over, axis=0, tiled=True)
    biases = [
        lax.dynamic_slice_in_dim(b, head_start, head_cols)[None] for b in (b_query, b_key, b_value)
    ]
    qkv_bias = pack(*biases)
    up_bias = lax.dynamic_slice_in_dim(b_up, up_start, hidden_cols)[None]

    def spread(v):
        half = jnp.concatenate([v, lax.ppermute(v, "gy", x_pairs)], axis=0)
        return half, lax.ppermute(half, "gy", core_pairs)

    def collect(keep, send):
        both = keep.astype(F32) + lax.ppermute(send, "gy", core_pairs).astype(F32)
        return both[:rows] + lax.ppermute(both[rows:].astype(BF16), "gy", x_pairs).astype(F32)

    def swap(blocks):
        return [blocks[0]] + [lax.ppermute(blocks[r], "gx", spins[r]) for r in range(1, gx)]

    quarter = HEAD_DIM // 4
    inverse = 10000.0 ** (-jnp.arange(quarter, dtype=F32) / quarter)
    places = position[:, :, 0, :].astype(F32)
    angles = jnp.concatenate(
        [inverse[None, :, None] * places[0][:, None], inverse[None, :, None] * places[1][:, None]],
        axis=1,
    )
    cos_all, sin_all = jnp.cos(angles), jnp.sin(angles)
    cos_own = lax.dynamic_slice_in_dim(cos_all, segment * qr, qr, 2)
    sin_own = lax.dynamic_slice_in_dim(sin_all, segment * qr, qr, 2)

    pictures, masks = picture[:, 0], patch_mask[:, 0]
    marks = jnp.where(masks == 1, pictures, 1000 + jnp.arange(slots, dtype=jnp.int32)[None])
    id_row = marks[:, None, :]
    id_col = jnp.broadcast_to(marks[:, :, None], (micros, slots, 128))
    nb = slots // BLK
    own_block = jnp.arange(nb, dtype=jnp.int32)[None]
    first_id, last_id = pictures[:, ::BLK], pictures[:, BLK - 1 :: BLK]
    below = jnp.sum(
        (pictures[:, None, :] < first_id[:, :, None]).astype(jnp.int32), axis=-1
    )
    upto = jnp.sum(
        (pictures[:, None, :] <= last_id[:, :, None]).astype(jnp.int32), axis=-1
    )
    low = jnp.where(masks[:, ::BLK] == 1, below // BLK, own_block)
    top = jnp.where(masks[:, BLK - 1 :: BLK] == 1, (upto - 1) // BLK, own_block)
    limits = jnp.stack([low, top], axis=1)

    tri = 3 * HEAD_DIM
    qkv_call = call(
        functools.partial(qkv_body, gx, dup, rows),
        [SM] + [VM] * 6,
        [((tri, qr), BF16)] * gx + [((qr, width), BF16)],
        [],
        2 * qr * width * gx * PACK,
        2 * (2 * qr * width + width * heads * PACK + gx * tri * qr),
        "qkv",
    )
    work = slots * slots // 2
    attend_call = call(
        functools.partial(attend_body, gx, slots),
        [SM, SM] + [VM] * (gx + 2),
        [((HEAD_DIM, qr), BF16)] * gx
        + [((tri, slots), BF16), ((1, slots), F32)],
        [((HEAD_DIM, slots), BF16), ((slots, HEAD_DIM), BF16)],
        4 * work * PACK,
        2 * 10 * HEAD_DIM * slots,
        "attend",
        work,
    )
    project_call = call(
        functools.partial(project_body, gx, dup, rows),
        [SM] + [VM] * (gx + 1),
        [((qr, head_cols), BF16), ((2 * rows, width), BF16), ((2 * rows, width), BF16)],
        [((head_cols, qr), BF16), ((qr, width), BF16)],
        2 * qr * width * head_cols,
        2 * (2 * qr * head_cols + width * head_cols + qr * width),
        "project",
    )
    half_rows = ((2 * rows, width), BF16)
    mlp_call = call(
        mlp_body,
        [VM] * 7,
        [((qr, hidden_cols), BF16)] * 2 + [half_rows] * 4 + [((1, hidden_cols), F32)],
        [],
        8 * qr * width * hidden_cols,
        2 * (4 * qr * width + 2 * width * hidden_cols + 2 * qr * hidden_cols),
        "mlp",
    )
    mix_grad_call = call(
        functools.partial(mix_grad_body, gx, dup, rows),
        [SM] + [VM] * 3,
        [((HEAD_DIM, qr), BF16)] * gx + [((qr, width), BF16)],
        [((head_cols, qr), BF16)],
        2 * qr * width * head_cols,
        2 * (2 * qr * width + width * head_cols + qr * head_cols),
        "mix_grad",
    )
    attend_back_call = call(
        functools.partial(attend_back_body, gx, slots),
        [SM, SM] + [VM] * (6 + gx),
        [((tri, qr), BF16)] * gx,
        [((HEAD_DIM, slots), BF16)]
        + [((slots, HEAD_DIM), BF16)] * 4
        + [((slots, BLK), F32)] * 2
        + [((slots, HEAD_DIM), F32)] * 2
        + [((tri, slots), BF16)],
        10 * work * PACK,
        2 * 10 * HEAD_DIM * slots,
        "attend_back",
        work,
    )
    qkv_back_call = call(
        functools.partial(qkv_back_body, gx, dup, rows),
        [SM] + [VM] * (gx + 1),
        [((qr, heads * PACK), BF16), half_rows, half_rows, ((1, heads * PACK), F32)],
        [((qr, width), BF16)],
        2 * qr * width * heads * PACK,
        2 * (2 * qr * heads * PACK + width * heads * PACK + qr * width),
        "qkv_back",
    )

    inputs = block_input[:, 0].astype(F32)
    normed = layer_norm(inputs, gain_attn, shift_attn)[0].astype(BF16)
    cots = out_grad[:, 0]
    normed_x = lax.ppermute(normed, "gy", x_pairs)
    cots_x = lax.ppermute(cots, "gy", x_pairs)
    saved = []
    for m in range(micros):
        na = jnp.concatenate([normed[m], normed_x[m]], axis=0)
        nb_half = lax.ppermute(na, "gy", core_pairs)
        *sent, rows_in = qkv_call(
            where, na, nb_half, full_qkv, qkv_bias, cos_own[m], sin_own[m]
        )
        *mixed, qkv_full, log_total = attend_call(
            where, limits[m], *swap(sent), id_row[m], id_col[m]
        )
        saved.append((rows_in, qkv_full, log_total, swap(mixed)))

    vec_gain_mlp = vec_shift_mlp = vec_up = vec_out = 0.0
    second = []
    outputs = []
    for m in range(micros):
        mix, keep, send = project_call(where, *saved[m][3], full_out)
        middle = inputs[m] + collect(keep, send) + b_out
        normed_two, normal_two, factor_two = layer_norm(middle, gain_mlp, shift_mlp)
        xa, xb = spread(normed_two.astype(BF16))
        ca = jnp.concatenate([cots[m], cots_x[m]], axis=0)
        cb = lax.ppermute(ca, "gy", core_pairs)
        act, hg, ra, rb, na, nb_half, up_part = mlp_call(
            xa, xb, ca, cb, full_up, full_down, up_bias
        )
        vec_up = vec_up + up_part[0]
        two_grad = collect(na, nb_half)
        result = collect(ra, rb)
        outputs.append((middle + result + b_down).astype(BF16))
        vec_gain_mlp = vec_gain_mlp + jnp.sum(two_grad * normal_two, axis=0)
        vec_shift_mlp = vec_shift_mlp + jnp.sum(two_grad, axis=0)
        middle_grad = cots[m].astype(F32) + norm_back(two_grad, normal_two, factor_two, gain_mlp)
        branch_grad = middle_grad.astype(BF16)
        vec_out = vec_out + jnp.sum(branch_grad.astype(F32), axis=0)
        second.append((mix, xa, xb, ca, cb, act, hg, middle_grad, branch_grad))

    vec_gain_attn = vec_shift_attn = vec_qkv = 0.0
    input_grads = []
    last = []
    for m in range(micros):
        middle_grad, branch_grad = second[m][7:]
        rows_in, qkv_full, log_total, _ = saved[m]
        ba, bb = spread(branch_grad)
        *sent, branch_rows = mix_grad_call(where, ba, bb, full_out)
        got = attend_back_call(
            where,
            limits[m],
            qkv_full,
            log_total,
            id_row[m],
            id_col[m],
            cos_all[m],
            sin_all[m],
            *swap(sent),
        )
        d, keep, send, part = qkv_back_call(where, *swap(got), full_qkv)
        vec_qkv = vec_qkv + part
        one_grad = collect(keep, send)
        _, normal_one, factor_one = layer_norm(inputs[m], gain_attn, shift_attn)
        vec_gain_attn = vec_gain_attn + jnp.sum(one_grad * normal_one, axis=0)
        vec_shift_attn = vec_shift_attn + jnp.sum(one_grad, axis=0)
        input_grads.append(middle_grad + norm_back(one_grad, normal_one, factor_one, gain_attn))
        last.append((rows_in, d, branch_rows))

    def reduce(full):
        return lax.psum_scatter(full, over, scatter_dimension=0, tiled=True).astype(F32)

    grad_up = reduce(
        weight_grad(
            [t for s in second for t in s[1:3]],
            [s[6][h * 2 * rows : (h + 1) * 2 * rows] for s in second for h in (0, 1)],
            "grad_up",
        )
    )
    grad_down = reduce(
        weight_grad(
            [t for s in second for t in s[3:5]],
            [s[5][h * 2 * rows : (h + 1) * 2 * rows] for s in second for h in (0, 1)],
            "grad_down",
        )
    )
    grad_out = reduce(weight_grad([t[2] for t in last], [s[0] for s in second], "grad_out"))
    grad_qkv = reduce(weight_grad([t[0] for t in last], [t[1] for t in last], "grad_qkv"))
    grad_query, grad_key, grad_value = unpack(grad_qkv)

    def whole(part, start, total):
        return lax.dynamic_update_slice_in_dim(jnp.zeros((total,), F32), part, start, 0)

    vec_q, vec_k, vec_v = [whole(t[0], head_start, b_query.shape[0]) for t in unpack(vec_qkv)]
    vectors = lax.psum(
        (
            vec_gain_attn,
            vec_shift_attn,
            vec_q,
            vec_k,
            vec_v,
            vec_out,
            vec_gain_mlp,
            vec_shift_mlp,
            whole(vec_up, up_start, b_up.shape[0]),
            jnp.sum(cots.astype(F32), axis=(0, 1)),
        ),
        ("dp", "gx", "gy"),
    )
    return (
        jnp.stack(outputs)[:, None],
        jnp.stack(input_grads)[:, None],
        vectors[0],
        vectors[1],
        grad_query,
        vectors[2],
        grad_key,
        vectors[3],
        grad_value,
        vectors[4],
        grad_out,
        vectors[5],
        vectors[6],
        vectors[7],
        grad_up,
        vectors[8],
        grad_down,
        vectors[9],
    )


def solution(mesh):
    acts = P(None, "dp", ("gx", "gy"), None)
    ids = P(None, "dp", None)
    weight = P(("dp", "gx"), "gy")
    placed = (acts, ids, P(None, None, "dp", None), ids, P(), P())
    placed += (weight, P()) * 4 + (P(), P()) + (weight, P()) * 2 + (acts,)
    outs = (acts, acts, P(), P()) + (weight, P()) * 4 + (P(), P()) + (weight, P()) * 2
    return jax.shard_map(
        per_device, mesh=mesh, in_specs=placed, out_specs=outs, check_vma=False
    )
```

time: 1810 us -> 963 us (0.53)
  waiting for transfers between devices: 1130 us -> 414 us
  matrix products: 311 us -> 0 us
  Pallas kernels: 0 us -> 242 us
  starting transfers between devices: 5.03 us -> 124 us
  blocking collectives: 156 us -> 43.8 us
  other arithmetic: 111 us -> 50.6 us
    reduce_scatter x23 -> x4, waiting for transfers between devices: 853 us -> 121 us  [reduce(): lax.psum_scatter(full, over, scatter_dimension=0, tiled=True).astype(F32)]
    dot_general x72 -> x0, matrix products: 311 us -> none  [the longest x3 41.6 us: per_device(): jnp.einsum('qrhd,krhd->rhqk', mixture_grad, values_all, preferred_element...]
    pallas_call x0 -> x25, Pallas kernels: none -> 242 us  [the longest x3 52.8 us: per_device(): attend_back_call(where, limits[m], qkv_full, log_total, id_row[m], id_col...]
    ppermute x0 -> x80, waiting for transfers between devices: none -> 161 us  [the longest x12 70.7 us: collect(): lax.ppermute(both[rows:].astype(BF16), 'gy', x_pairs).astype(F32)]
    all_gather x20 -> x3, waiting for transfers between devices: 150 us -> 0.01 us  [the longest x1 0.01 us: per_device(): lax.all_gather(pack(w_query, w_key, w_value), over, axis=0, tiled=True)]
    psum x1, waiting for transfers between devices: 0.01 us -> 131 us  [per_device(): lax.psum((vec_gain_attn, vec_shift_attn, vec_q, vec_k, vec_v, vec_out, ve...]
    unnamed x46 -> x8, waiting for transfers between devices: 131 us -> 0.81 us
    ppermute x0 -> x80, starting transfers between devices: none -> 124 us  [the longest x36 92.8 us: swap(): lax.ppermute(blocks[r], 'gx', spins[r])]
  transfers between devices with their start and end apart: 45 -> 88, of which waited for: 28 -> 26; matrix products, arithmetic and copies ran while one was open for 24% -> 9% of each run, Pallas kernels for 0% -> 24%
where the time goes in v1:
time: 963 us; the launch traced here: 953 us
  waiting for transfers between devices  414 us (43%)
  Pallas kernels  242 us (25%)
  starting transfers between devices  124 us (13%)
  local copies, waits for them, and re-layouts  61.9 us (6%)
  other arithmetic  50.6 us (5%)
  blocking collectives  43.8 us (5%)
  between operations  15.9 us (2%)
    psum x1, waiting for transfers between devices, per_device(): lax.psum((vec_gain_attn, vec_shift_attn, vec_q, vec_k, vec_v, vec_out, ve...  131 us
    reduce_scatter x4, waiting for transfers between devices, reduce(): lax.psum_scatter(full, over, scatter_dimension=0, tiled=True).astype(F32)  121 us
    ppermute x36, starting transfers between devices, swap(): lax.ppermute(blocks[r], 'gx', spins[r])  92.8 us
    ppermute x12, waiting for transfers between devices, collect(): lax.ppermute(both[rows:].astype(BF16), 'gy', x_pairs).astype(F32)  70.7 us
    pallas_call x3, Pallas kernels, per_device(): attend_back_call(where, limits[m], qkv_full, log_total, id_row[m], id_col...  52.8 us
    ppermute x36, waiting for transfers between devices, swap(): lax.ppermute(blocks[r], 'gx', spins[r])  51.2 us
    pallas_call x3, Pallas kernels, per_device(): mlp_call(xa, xb, ca, cb, full_up, full_down, up_bias)  51.1 us
    all_gather x1, blocking collectives, per_device(): full_out = lax.all_gather(w_out, over, axis=0, tiled=True)  43.8 us
  transfers between devices with their start and end apart: 88, of which 26 were waited for; matrix products, arithmetic and copies ran while one was open for 9% of the time, Pallas kernels for 24%

profile of v1, /device:TPU:0, one launch (start us, length us, event | category | flops | bytes accessed | tf_op | source)
XLA Modules:
  0.0 952.7 jit_solution(13272783476054353025)
XLA Ops:
  14.7 3.0 collective-permute-start
  21.5 43.8 %all_gather.13.rest_4_.wo = bf16[1280,320]{1,0:T(8,128)(2,1)} all-gather(bf16[160,320]{1,0:T(8,128)(2,1)S(1)} %copy-done.45), channel_id=1, replica_groups=mesh['dp'=2,'gx'=4,'gy'=4] {'dp','gx'}, dimensions={0}, use_global_device_ids=true | all-gather | bytes 921600 | tf_op jit(solution)/shard_map/all_gather | solution.py:389
  65.8 4.5 fusion
  80.6 5.2 qkv.3
  90.7 5.2 qkv.4
  100.1 9.0 collective-permute-start.18
  109.1 9.3 collective-permute-done.3.rest_2_
  118.4 15.4 %collective-permute-start.19 = (bf16[240,512]{1,0:T(8,128)(2,1)}, bf16[240,512]{1,0:T(8,128)(2,1)S(1)}, u32[]{:S(2)}, u32[]{:S(2)}) collective-permute-start(bf16[240,512]{1,0:T(8,128)(2,1)} %get-tuple-element.135), channel_id=1, source_target_pairs={{0,12},{4,0},{8,4},{12,8},{1,13},{5,1},{9,5},{13,9},{2,14},{6,2},{... | collective-permute-start | bytes 737288 | tf_op jit(solution)/shard_map/ppermute | solution.py:407
  135.1 14.6 %attend.3 = (bf16[80,512]{1,0:T(8,128)(2,1)}, bf16[80,512]{1,0:T(8,128)(2,1)}, bf16[80,512]{1,0:T(8,128)(2,1)}, bf16[80,512]{1,0:T(8,128)(2,1)}, bf16[240,2048]{1,0:T(8,128)(2,1)}, /*index=5*/f32[1,2048]{1,0:T(1,128)}) custom-call(s32[2]{0:T(128)} %pad_add_fusion.3.s_ref, s32[2,8]{1,0:T(2,128)} %bitcast.180, bf16[240,512]{1,0:T(8,128)(2,1)} %get-tuple-element.120.rest_0_, ...), custom_call_target="tpu_custom_call" | custom-call | flops 2147483648 | bytes 3276800 | tf_op jit(solution)/shard_map/attend/pallas_call | solution.py:523
  154.7 5.3 qkv.5
  160.0 6.1 collective-permute-start.31
  166.1 19.4 %collective-permute-done.6.rest_2_ = bf16[80,512]{1,0:T(8,128)(2,1)S(1)} collective-permute-done((bf16[80,512]{1,0:T(8,128)(2,1)}, bf16[80,512]{1,0:T(8,128)(2,1)S(1)}, u32[]{:S(2)}, u32[]{:S(2)}) %collective-permute-start.6) | collective-permute-done | bytes 81952 | tf_op jit(solution)/shard_map/ppermute | solution.py:407
  186.8 3.5 project.3
  191.7 13.7 %attend.4 = (bf16[80,512]{1,0:T(8,128)(2,1)}, bf16[80,512]{1,0:T(8,128)(2,1)}, bf16[80,512]{1,0:T(8,128)(2,1)}, bf16[80,512]{1,0:T(8,128)(2,1)}, bf16[240,2048]{1,0:T(8,128)(2,1)}, /*index=5*/f32[1,2048]{1,0:T(1,128)}) custom-call(s32[2]{0:T(128)} %pad_add_fusion.3.s_ref, s32[2,8]{1,0:T(2,128)} %bitcast.176, bf16[240,512]{1,0:T(8,128)(2,1)} %get-tuple-element.132.rest_0_, ...), custom_call_target="tpu_custom_call" | custom-call | flops 2147483648 | bytes 3276800 | tf_op jit(solution)/shard_map/attend/pallas_call | solution.py:523
  205.4 3.9 collective-permute-start.20
  210.8 2.8 collective-permute-start.22
  215.0 14.5 %attend.5 = (bf16[80,512]{1,0:T(8,128)(2,1)}, bf16[80,512]{1,0:T(8,128)(2,1)}, bf16[80,512]{1,0:T(8,128)(2,1)}, bf16[80,512]{1,0:T(8,128)(2,1)}, bf16[240,2048]{1,0:T(8,128)(2,1)}, /*index=5*/f32[1,2048]{1,0:T(1,128)}) custom-call(s32[2]{0:T(128)} %pad_add_fusion.3.s_ref, s32[2,8]{1,0:T(2,128)} %bitcast.178, bf16[240,512]{1,0:T(8,128)(2,1)} %get-tuple-element.144.rest_0_, ...), custom_call_target="tpu_custom_call" | custom-call | flops 2147483648 | bytes 3276800 | tf_op jit(solution)/shard_map/attend/pallas_call | solution.py:523
  230.2 3.3 collective-permute-start.36
  233.5 3.5 project.4
  240.0 3.0 collective-permute-done.35.rest_2_
  243.7 3.4 project.5
  254.1 9.1 collective-permute-done.12
  264.4 5.7 collective-permute-done.9
  270.1 7.0 collective-permute-done.24
  277.1 6.5 collective-permute-done.38
  290.6 5.4 collective-permute-done.39
  297.8 5.2 collective-permute-done.25
  303.9 4.8 collective-permute-done.10
  311.0 17.1 %mlp.5 = (bf16[512,1280]{1,0:T(8,128)(2,1)}, bf16[512,1280]{1,0:T(8,128)(2,1)}, bf16[256,1280]{1,0:T(8,128)(2,1)}, bf16[256,1280]{1,0:T(8,128)(2,1)}, bf16[256,1...) custom-call(bf16[256,1280]{1,0:T(8,128)(2,1)} %pad_maximum_fusion.8.xa.rest_4_, ...), custom_call_target="tpu_custom_call" | custom-call | flops 6710886400 | bytes 14417920 | tf_op jit(solution)/shard_map/mlp/pallas_call | solution.py:538
  328.6 17.0 %mlp.4 = (bf16[512,1280]{1,0:T(8,128)(2,1)}, bf16[512,1280]{1,0:T(8,128)(2,1)}, bf16[256,1280]{1,0:T(8,128)(2,1)}, bf16[256,1280]{1,0:T(8,128)(2,1)}, bf16[256,1...) custom-call(bf16[256,1280]{1,0:T(8,128)(2,1)} %pad_maximum_fusion.5.xa.rest_2_, ...), custom_call_target="tpu_custom_call" | custom-call | flops 6710886400 | bytes 14417920 | tf_op jit(solution)/shard_map/mlp/pallas_call | solution.py:538
  346.1 17.0 %mlp.3 = (bf16[512,1280]{1,0:T(8,128)(2,1)}, bf16[512,1280]{1,0:T(8,128)(2,1)}, bf16[256,1280]{1,0:T(8,128)(2,1)}, bf16[256,1280]{1,0:T(8,128)(2,1)}, bf16[256,1...) custom-call(bf16[256,1280]{1,0:T(8,128)(2,1)} %pad_maximum_fusion.2.xa.rest_0_, ...), custom_call_target="tpu_custom_call" | custom-call | flops 6710886400 | bytes 14417920 | tf_op jit(solution)/shard_map/mlp/pallas_call | solution.py:538
  375.6 27.4 %collective-permute-done.45 = bf16[128,1280]{1,0:T(8,128)(2,1)S(1)} collective-permute-done((bf16[128,1280]{1,0:T(8,128)(2,1)S(1)}, bf16[128,1280]{1,0:T(8,128)(2,1)S(1)}, u32[]{:S(2)}, u32[]{:S(2)}) %collective-permute-start.45) | collective-permute-done | bytes 327712 | tf_op jit(solution)/shard_map/ppermute | solution.py:404
  405.0 6.9 collective-permute-done.15
  420.3 3.2 collective-permute-done.46
  423.7 6.9 collective-permute-done.70
  430.7 4.6 collective-permute-done.58
  435.5 3.9 mix_grad.3
  439.4 3.8 mix_grad.5
  443.2 3.8 mix_grad.4
  447.0 6.8 grad_out.1
  458.6 11.1 %grad_up.1 = bf16[1280,1280]{1,0:T(8,128)(2,1)} custom-call(bf16[256,1280]{1,0:T(8,128)(2,1)} %pad_maximum_fusion.2.xa.rest_0_, bf16[256,1280]{1,0:T(8,128)(2,1)} %collective-permute-done.11.xb.rest_1_, bf16[256,1280]{1,0:T(8,128)(2,1)} %pad_maximum_fusion.5.xa.rest_2_, bf16[256,1280]{1,0:T(8,128)(2,1)} %collective-permute-done.26.xb.rest_3_, ...), custom_call_target="tpu_custom_call" | custom-call | flops 5033164800 | bytes 11141120 | tf_op jit(solution)/shard_map/grad_up/pallas_call | solution.py:305
  475.8 11.2 %grad_down.1 = bf16[1280,1280]{1,0:T(8,128)(2,1)} custom-call(bf16[256,1280]{1,0:T(8,128)(2,1)} %pad_maximum_fusion.3.ca.rest_0_, bf16[256,1280]{1,0:T(8,128)(2,1)} %collective-permute-done.13.cb.rest_1_, bf16[256,1280]{1,0:T(8,128)(2,1)} %pad_maximum_fusion.6.ca.rest_2_, bf16[256,1280]{1,0:T(8,128)(2,1)} %collective-permute-done.27.cb.rest_3_, ...), custom_call_target="tpu_custom_call" | custom-call | flops 5033164800 | bytes 11141120 | tf_op jit(solution)/shard_map/grad_down/pallas_call | solution.py:305
  496.7 2.9 collective-permute-start.50
  504.2 3.5 collective-permute-done.49.rest_8_
  507.8 4.0 collective-permute-start.61
  511.8 17.9 %attend_back.3 = (bf16[240,512]{1,0:T(8,128)(2,1)}, bf16[240,512]{1,0:T(8,128)(2,1)}, bf16[240,512]{1,0:T(8,128)(2,1)}, bf16[240,512]{1,0:T(8,128)(2,1)}) custom-call(s32[2]{0:T(128)} %pad_add_fusion.3.s_ref, s32[2,8]{1,0:T(2,128)} %bitcast.181, bf16[240,2048]{1,0:T(8,128)(2,1)} %get-tuple-element.158.rest_0_, f32[1,2048]{1,0:T(1,128)} %get-tuple-element.159.rest_1_, ...), custom_call_target="tpu_custom_call" | custom-call | flops 5368709120 | bytes 3276800 | tf_op jit(solution)/shard_map/attend_back/pallas_call | solution.py:560
  532.8 18.0 %attend_back.5 = (bf16[240,512]{1,0:T(8,128)(2,1)}, bf16[240,512]{1,0:T(8,128)(2,1)}, bf16[240,512]{1,0:T(8,128)(2,1)}, bf16[240,512]{1,0:T(8,128)(2,1)}) custom-call(s32[2]{0:T(128)} %pad_add_fusion.3.s_ref, s32[2,8]{1,0:T(2,128)} %bitcast.179, bf16[240,2048]{1,0:T(8,128)(2,1)} %get-tuple-element.186.rest_0_, f32[1,2048]{1,0:T(1,128)} %get-tuple-element.187.rest_1_, ...), custom_call_target="tpu_custom_call" | custom-call | flops 5368709120 | bytes 3276800 | tf_op jit(solution)/shard_map/attend_back/pallas_call | solution.py:560
  550.8 3.8 collective-permute-start.53
  556.6 2.9 collective-permute-start.77
  559.5 16.9 %attend_back.4 = (bf16[240,512]{1,0:T(8,128)(2,1)}, bf16[240,512]{1,0:T(8,128)(2,1)}, bf16[240,512]{1,0:T(8,128)(2,1)}, bf16[240,512]{1,0:T(8,128)(2,1)}) custom-call(s32[2]{0:T(128)} %pad_add_fusion.3.s_ref, s32[2,8]{1,0:T(2,128)} %bitcast.177, bf16[240,2048]{1,0:T(8,128)(2,1)} %get-tuple-element.172.rest_0_, f32[1,2048]{1,0:T(1,128)} %get-tuple-element.173.rest_1_, ...), custom_call_target="tpu_custom_call" | custom-call | flops 5368709120 | bytes 3276800 | tf_op jit(solution)/shard_map/attend_back/pallas_call | solution.py:560
  576.8 11.7 %collective-permute-start.64 = (bf16[240,512]{1,0:T(8,128)(2,1)}, bf16[240,512]{1,0:T(8,128)(2,1)S(1)}, u32[]{:S(2)}, u32[]{:S(2)}) collective-permute-start(bf16[240,512]{1,0:T(8,128)(2,1)} %get-tuple-element.180), channel_id=1, source_target_pairs={{0,8},{4,12},{8,0},{12,4},{1,9},{5,13},{9,1},{13,5},{2,10},{6,14},... | collective-permute-start | bytes 737288 | tf_op jit(solution)/shard_map/ppermute | solution.py:407
  588.5 4.3 collective-permute-start.65
  592.8 6.5 qkv_back.3
  599.3 10.0 %collective-permute-done.76.rest_2_ = bf16[240,512]{1,0:T(8,128)(2,1)S(1)} collective-permute-done((bf16[240,512]{1,0:T(8,128)(2,1)}, bf16[240,512]{1,0:T(8,128)(2,1)S(1)}, u32[]{:S(2)}, u32[]{:S(2)}) %collective-permute-start.76) | collective-permute-done | bytes 245792 | tf_op jit(solution)/shard_map/ppermute | solution.py:407
  610.0 6.3 qkv_back.5
  616.9 3.0 collective-permute-done.64.rest_2_
  620.6 6.4 qkv_back.4
  627.7 9.7 %grad_qkv.1 = bf16[1280,1024]{1,0:T(8,128)(2,1)} custom-call(bf16[512,1280]{1,0:T(8,128)(2,1)} %get-tuple-element.198.rest_0_, bf16[512,1280]{1,0:T(8,128)(2,1)} %get-tuple-element.199.rest_1_, bf16[512,1280]{1,0:T(8,128)(2,1)} %get-tuple-element.200.rest_2_, bf16[512,1024]{1,0:T(8,128)(2,1)} %get-tuple-element.201.rest_3_, ...), custom_call_target="tpu_custom_call" | custom-call | flops 4026531840 | bytes 9699328 | tf_op jit(solution)/shard_map/grad_qkv/pallas_call | solution.py:305
  646.2 4.2 collective-permute-done.55
  651.0 6.4 collective-permute-done.79
  657.4 6.5 collective-permute-done.67
  674.2 49.6 %reduce-scatter.11.cloned.1.call-done = bf16[160,1280]{1,0:T(8,128)(2,1)} async-done(((bf16[1280,1280]{1,0:T(8,128)(2,1)}), bf16[160,1280]{1,0:T(8,128)(2,1)}) %reduce-scatter.11.cloned.1.call-update) | async-done | bytes 409616 | tf_op jit(solution)/shard_map/reduce_scatter | solution.py:581
  725.7 71.3 %reduce-scatter.5.cloned.1.call-done = bf16[160,1024]{1,0:T(8,128)(2,1)} async-done(((bf16[1280,1024]{1,0:T(8,128)(2,1)}), bf16[160,1024]{1,0:T(8,128)(2,1)}) %reduce-scatter.5.cloned.1.call-update) | async-done | bytes 327696 | tf_op jit(solution)/shard_map/reduce_scatter | solution.py:581
  801.4 131.1 %all-reduce.3.cloned.1.call-done = (f32[1280]{0:T(1024)}, f32[1280]{0:T(1024)}, f32[1280]{0:T(1024)}, f32[1280]{0:T(1024)}, f32[1280]{0:T(1024)}, /*index=5*/f32...) async-done(((f32[1280]{0:T(1024)}, f32[1280]{0:T(1024)}, f32[1280]{0:T(1024)}, f32[1280]{0:T(1024)}, f32[1280]{0:T(1024)}, ...) | async-done | bytes 66576 | tf_op jit(solution)/shard_map/psum | solution.py:605
  (515 shorter events, 163.1 us)
Async XLA Ops:
  7.2 73.4 %all-gather.4.cloned.1.call-start = ((), (), s32[]{:S(2)}) async-start(), calls=%async_computation.4 | async-start | bytes 2949120 | tf_op jit(solution)/shard_map/all_gather | solution.py:388
  11.9 299.1 %all-gather.6.cloned.1.call-start = ((), (), s32[]{:S(2)}) async-start(), calls=%async_computation.5 | async-start | bytes 3686400 | tf_op jit(solution)/shard_map/all_gather | solution.py:390
  12.6 298.4 %all-gather.8.cloned.1.call-start = ((), (), s32[]{:S(2)}) async-start(), calls=%async_computation.6 | async-start | bytes 3686400 | tf_op jit(solution)/shard_map/all_gather | solution.py:391
  14.7 60.0 %collective-permute-start = (bf16[3,128,1280]{2,1,0:T(8,128)(2,1)}, bf16[3,128,1280]{2,1,0:T(8,128)(2,1)}, u32[]{:S(2)}, u32[]{:S(2)}) collective-permute-start(bf16[3,128,1280]{2,1,0:T(8,128)(2,1)} %add_convert_fusion), channel_id=1, source_target_pairs={{0,2},{1,3},{2,0},{3,1},{4,6},{5,7},{6,4},{7,5},{8,10},{9,11},{10,... | collective-permute-start | bytes 2949128 | tf_op jit(solution)/shard_map/ppermute | solution.py:514
  17.7 652.8 %reduce-scatter.7.cloned.1.call-start = ((), (), s32[]{:S(2)}) async-start(), calls=%async_computation.8 | async-start | bytes 1105920 | tf_op jit(solution)/shard_map/reduce_scatter | solution.py:581
  80.6 71.7 %collective-permute-start.30 = (bf16[256,1280]{1,0:T(8,128)(2,1)}, bf16[256,1280]{1,0:T(8,128)(2,1)}, u32[]{:S(2)}, u32[]{:S(2)}) collective-permute-start(bf16[256,1280]{1,0:T(8,128)(2,1)} %pad_maximum_fusion.7.xa), channel_id=1, source_target_pairs={{0,1},{1,0},{2,3},{3,2},{4,5},{5,4},{6,7},{7,6},{8,9},{9,8},{10,11... | collective-permute-start | bytes 1966088 | tf_op jit(solution)/shard_map/ppermute | solution.py:519
  86.5 31.9 %collective-permute-start.3 = (bf16[240,512]{1,0:T(8,128)(2,1)}, bf16[240,512]{1,0:T(8,128)(2,1)}, u32[]{:S(2)}, u32[]{:S(2)}) collective-permute-start(bf16[240,512]{1,0:T(8,128)(2,1)} %get-tuple-element.122), channel_id=1, source_target_pairs={{0,8},{4,12},{8,0},{12,4},{1,9},{5,13},{9,1},{13,5},{2,10},{6,14},... | collective-permute-start | bytes 737288 | tf_op jit(solution)/shard_map/ppermute | solution.py:407
  89.0 44.8 %collective-permute-start.4 = (bf16[240,512]{1,0:T(8,128)(2,1)}, bf16[240,512]{1,0:T(8,128)(2,1)}, u32[]{:S(2)}, u32[]{:S(2)}) collective-permute-start(bf16[240,512]{1,0:T(8,128)(2,1)} %get-tuple-element.123), channel_id=1, source_target_pairs={{0,12},{4,0},{8,4},{12,8},{1,13},{5,1},{9,5},{13,9},{2,14},{6,2},{... | collective-permute-start | bytes 737288 | tf_op jit(solution)/shard_map/ppermute | solution.py:407
  95.9 56.4 %collective-permute-start.17 = (bf16[240,512]{1,0:T(8,128)(2,1)}, bf16[240,512]{1,0:T(8,128)(2,1)S(1)}, u32[]{:S(2)}, u32[]{:S(2)}) collective-permute-start(bf16[240,512]{1,0:T(8,128)(2,1)} %get-tuple-element.133), channel_id=1, source_target_pairs={{0,4},{4,8},{8,12},{12,0},{1,5},{5,9},{9,13},{13,1},{2,6},{6,10},{... | collective-permute-start | bytes 737288 | tf_op jit(solution)/shard_map/ppermute | solution.py:407
  100.1 90.1 %collective-permute-start.18 = (bf16[240,512]{1,0:T(8,128)(2,1)}, bf16[240,512]{1,0:T(8,128)(2,1)S(1)}, u32[]{:S(2)}, u32[]{:S(2)}) collective-permute-start(bf16[240,512]{1,0:T(8,128)(2,1)} %get-tuple-element.134), channel_id=1, source_target_pairs={{0,8},{4,12},{8,0},{12,4},{1,9},{5,13},{9,1},{13,5},{2,10},{6,14},... | collective-permute-start | bytes 737288 | tf_op jit(solution)/shard_map/ppermute | solution.py:407
  118.4 71.9 %collective-permute-start.19 = (bf16[240,512]{1,0:T(8,128)(2,1)}, bf16[240,512]{1,0:T(8,128)(2,1)S(1)}, u32[]{:S(2)}, u32[]{:S(2)}) collective-permute-start(bf16[240,512]{1,0:T(8,128)(2,1)} %get-tuple-element.135), channel_id=1, source_target_pairs={{0,12},{4,0},{8,4},{12,8},{1,13},{5,1},{9,5},{13,9},{2,14},{6,2},{... | collective-permute-start | bytes 737288 | tf_op jit(solution)/shard_map/ppermute | solution.py:407
  152.3 33.2 %collective-permute-start.6 = (bf16[80,512]{1,0:T(8,128)(2,1)}, bf16[80,512]{1,0:T(8,128)(2,1)S(1)}, u32[]{:S(2)}, u32[]{:S(2)}) collective-permute-start(bf16[80,512]{1,0:T(8,128)(2,1)} %get-tuple-element.126), channel_id=1, source_target_pairs={{0,8},{4,12},{8,0},{12,4},{1,9},{5,13},{9,1},{13,5},{2,10},{6,14},... | collective-permute-start | bytes 245768 | tf_op jit(solution)/shard_map/ppermute | solution.py:407
  152.3 33.1 %collective-permute-start.7 = (bf16[80,512]{1,0:T(8,128)(2,1)}, bf16[80,512]{1,0:T(8,128)(2,1)S(1)}, u32[]{:S(2)}, u32[]{:S(2)}) collective-permute-start(bf16[80,512]{1,0:T(8,128)(2,1)} %get-tuple-element.127), channel_id=1, source_target_pairs={{0,12},{4,0},{8,4},{12,8},{1,13},{5,1},{9,5},{13,9},{2,14},{6,2},{... | collective-permute-start | bytes 245768 | tf_op jit(solution)/shard_map/ppermute | solution.py:407
  160.0 49.3 %collective-permute-start.31 = (bf16[240,512]{1,0:T(8,128)(2,1)}, bf16[240,512]{1,0:T(8,128)(2,1)S(1)}, u32[]{:S(2)}, u32[]{:S(2)}) collective-permute-start(bf16[240,512]{1,0:T(8,128)(2,1)} %get-tuple-element.145), channel_id=1, source_target_pairs={{0,4},{4,8},{8,12},{12,0},{1,5},{5,9},{9,13},{13,1},{2,6},{6,10},{... | collective-permute-start | bytes 737288 | tf_op jit(solution)/shard_map/ppermute | solution.py:407
  185.4 25.4 %collective-permute-start.32 = (bf16[240,512]{1,0:T(8,128)(2,1)}, bf16[240,512]{1,0:T(8,128)(2,1)S(1)}, u32[]{:S(2)}, u32[]{:S(2)}) collective-permute-start(bf16[240,512]{1,0:T(8,128)(2,1)} %get-tuple-element.146), channel_id=1, source_target_pairs={{0,8},{4,12},{8,0},{12,4},{1,9},{5,13},{9,1},{13,5},{2,10},{6,14},... | collective-permute-start | bytes 737288 | tf_op jit(solution)/shard_map/ppermute | solution.py:407
  186.1 27.6 %collective-permute-start.33 = (bf16[240,512]{1,0:T(8,128)(2,1)}, bf16[240,512]{1,0:T(8,128)(2,1)S(1)}, u32[]{:S(2)}, u32[]{:S(2)}) collective-permute-start(bf16[240,512]{1,0:T(8,128)(2,1)} %get-tuple-element.147), channel_id=1, source_target_pairs={{0,12},{4,0},{8,4},{12,8},{1,13},{5,1},{9,5},{13,9},{2,14},{6,2},{... | collective-permute-start | bytes 737288 | tf_op jit(solution)/shard_map/ppermute | solution.py:407
  190.2 56.9 %collective-permute-start.8 = (bf16[256,1280]{1,0:T(8,128)(2,1)}, bf16[256,1280]{1,0:T(8,128)(2,1)}, u32[]{:S(2)}, u32[]{:S(2)}) collective-permute-start(bf16[256,1280]{1,0:T(8,128)(2,1)} %get-tuple-element.129), channel_id=1, source_target_pairs={{0,1},{1,0},{2,3},{3,2},{4,5},{5,4},{6,7},{7,6},{8,9},{9,8},{10,11... | collective-permute-start | bytes 1966088 | tf_op jit(solution)/shard_map/ppermute | solution.py:403
  205.4 24.2 %collective-permute-start.20 = (bf16[80,512]{1,0:T(8,128)(2,1)}, bf16[80,512]{1,0:T(8,128)(2,1)S(1)}, u32[]{:S(2)}, u32[]{:S(2)}) collective-permute-start(bf16[80,512]{1,0:T(8,128)(2,1)} %get-tuple-element.137), channel_id=1, source_target_pairs={{0,4},{4,8},{8,12},{12,0},{1,5},{5,9},{9,13},{13,1},{2,6},{6,10},{... | collective-permute-start | bytes 245768 | tf_op jit(solution)/shard_map/ppermute | solution.py:407
  209.3 20.9 %collective-permute-start.21 = (bf16[80,512]{1,0:T(8,128)(2,1)}, bf16[80,512]{1,0:T(8,128)(2,1)S(1)}, u32[]{:S(2)}, u32[]{:S(2)}) collective-permute-start(bf16[80,512]{1,0:T(8,128)(2,1)} %get-tuple-element.138), channel_id=1, source_target_pairs={{0,8},{4,12},{8,0},{12,4},{1,9},{5,13},{9,1},{13,5},{2,10},{6,14},... | collective-permute-start | bytes 245768 | tf_op jit(solution)/shard_map/ppermute | solution.py:407
  210.8 22.6 %collective-permute-start.22 = (bf16[80,512]{1,0:T(8,128)(2,1)}, bf16[80,512]{1,0:T(8,128)(2,1)}, u32[]{:S(2)}, u32[]{:S(2)}) collective-permute-start(bf16[80,512]{1,0:T(8,128)(2,1)} %get-tuple-element.139), channel_id=1, source_target_pairs={{0,12},{4,0},{8,4},{12,8},{1,13},{5,1},{9,5},{13,9},{2,14},{6,2},{... | collective-permute-start | bytes 245768 | tf_op jit(solution)/shard_map/ppermute | solution.py:407
  238.4 24.8 %collective-permute-start.12 = (bf16[3,128,1280]{2,1,0:T(8,128)(2,1)S(1)}, bf16[3,128,1280]{2,1,0:T(8,128)(2,1)}, u32[]{:S(2)}, u32[]{:S(2)}) collective-permute-start(bf16[3,128,1280]{2,1,0:T(8,128)(2,1)S(1)} %bitcast.161), channel_id=1, source_target_pairs={{0,2},{1,3},{2,0},{3,1},{4,6},{5,7},{6,4},{7,5},{8,10},{9,11},{10,... | collective-permute-start | bytes 2949128 | tf_op jit(solution)/shard_map/ppermute | solution.py:515
  248.6 21.4 %collective-permute-start.9 = (bf16[128,1280]{1,0:T(8,128)(2,1)S(1)}, bf16[128,1280]{1,0:T(8,128)(2,1)S(1)}, u32[]{:S(2)}, u32[]{:S(2)}) collective-permute-start(bf16[128,1280]{1,0:T(8,128)(2,1)S(1)} %slice.621), channel_id=1, source_target_pairs={{0,2},{1,3},{2,0},{3,1},{4,6},{5,7},{6,4},{7,5},{8,10},{9,11},{10,... | collective-permute-start | bytes 983048 | tf_op jit(solution)/shard_map/ppermute | solution.py:404
  251.7 25.4 %collective-permute-start.24 = (bf16[128,1280]{1,0:T(8,128)(2,1)S(1)}, bf16[128,1280]{1,0:T(8,128)(2,1)S(1)}, u32[]{:S(2)}, u32[]{:S(2)}) collective-permute-start(bf16[128,1280]{1,0:T(8,128)(2,1)S(1)} %slice.619), channel_id=1, source_target_pairs={{0,2},{1,3},{2,0},{3,1},{4,6},{5,7},{6,4},{7,5},{8,10},{9,11},{10,... | collective-permute-start | bytes 983048 | tf_op jit(solution)/shard_map/ppermute | solution.py:404
  252.3 31.3 %collective-permute-start.38 = (bf16[128,1280]{1,0:T(8,128)(2,1)S(1)}, bf16[128,1280]{1,0:T(8,128)(2,1)S(1)}, u32[]{:S(2)}, u32[]{:S(2)}) collective-permute-start(bf16[128,1280]{1,0:T(8,128)(2,1)S(1)} %slice.617), channel_id=1, source_target_pairs={{0,2},{1,3},{2,0},{3,1},{4,6},{5,7},{6,4},{7,5},{8,10},{9,11},{10,... | collective-permute-start | bytes 983048 | tf_op jit(solution)/shard_map/ppermute | solution.py:404
  287.1 22.6 %collective-permute-start.41 = (bf16[256,1280]{1,0:T(8,128)(2,1)S(1)}, bf16[256,1280]{1,0:T(8,128)(2,1)S(1)}, u32[]{:S(2)}, u32[]{:S(2)}) collective-permute-start(bf16[256,1280]{1,0:T(8,128)(2,1)S(1)} %pad_maximum_fusion.9.ca.rest_4_), channel_id=1, source_target_pairs={{0,1},{1,0},{2,3},{3,2},{4,5},{5,4},{6,7},{7,6},{8,9},{9,8},{10,11... | collective-permute-start | bytes 1966088 | tf_op jit(solution)/shard_map/ppermute | solution.py:537
  288.1 40.1 %collective-permute-start.27 = (bf16[256,1280]{1,0:T(8,128)(2,1)}, bf16[256,1280]{1,0:T(8,128)(2,1)}, u32[]{:S(2)}, u32[]{:S(2)}) collective-permute-start(bf16[256,1280]{1,0:T(8,128)(2,1)} %pad_maximum_fusion.6.ca.rest_2_), channel_id=1, source_target_pairs={{0,1},{1,0},{2,3},{3,2},{4,5},{5,4},{6,7},{7,6},{8,9},{9,8},{10,11... | collective-permute-start | bytes 1966088 | tf_op jit(solution)/shard_map/ppermute | solution.py:537
  289.0 19.7 %collective-permute-start.10 = (bf16[128,1280]{1,0:T(8,128)(2,1)S(1)}, bf16[128,1280]{1,0:T(8,128)(2,1)S(1)}, u32[]{:S(2)}, u32[]{:S(2)}) collective-permute-start(bf16[128,1280]{1,0:T(8,128)(2,1)S(1)} %get-tuple-element.419), channel_id=1, source_target_pairs={{0,2},{1,3},{2,0},{3,1},{4,6},{5,7},{6,4},{7,5},{8,10},{9,11},{10,... | collective-permute-start | bytes 983048 | tf_op jit(solution)/shard_map/ppermute | solution.py:399
  303.0 42.6 %collective-permute-start.13 = (bf16[256,1280]{1,0:T(8,128)(2,1)}, bf16[256,1280]{1,0:T(8,128)(2,1)}, u32[]{:S(2)}, u32[]{:S(2)}) collective-permute-start(bf16[256,1280]{1,0:T(8,128)(2,1)} %pad_maximum_fusion.3.ca.rest_0_), channel_id=1, source_target_pairs={{0,1},{1,0},{2,3},{3,2},{4,5},{5,4},{6,7},{7,6},{8,9},{9,8},{10,11... | collective-permute-start | bytes 1966088 | tf_op jit(solution)/shard_map/ppermute | solution.py:537
  308.7 19.9 %collective-permute-start.26 = (bf16[256,1280]{1,0:T(8,128)(2,1)}, bf16[256,1280]{1,0:T(8,128)(2,1)}, u32[]{:S(2)}, u32[]{:S(2)}) collective-permute-start(bf16[256,1280]{1,0:T(8,128)(2,1)} %pad_maximum_fusion.5.xa.rest_2_), channel_id=1, source_target_pairs={{0,1},{1,0},{2,3},{3,2},{4,5},{5,4},{6,7},{7,6},{8,9},{9,8},{10,11... | collective-permute-start | bytes 1966088 | tf_op jit(solution)/shard_map/ppermute | solution.py:400
  310.5 35.6 %collective-permute-start.11 = (bf16[256,1280]{1,0:T(8,128)(2,1)}, bf16[256,1280]{1,0:T(8,128)(2,1)}, u32[]{:S(2)}, u32[]{:S(2)}) collective-permute-start(bf16[256,1280]{1,0:T(8,128)(2,1)} %pad_maximum_fusion.2.xa.rest_0_), channel_id=1, source_target_pairs={{0,1},{1,0},{2,3},{3,2},{4,5},{5,4},{6,7},{7,6},{8,9},{9,8},{10,11... | collective-permute-start | bytes 1966088 | tf_op jit(solution)/shard_map/ppermute | solution.py:400
  328.1 35.1 %collective-permute-start.68 = (bf16[256,1280]{1,0:T(8,128)(2,1)}, bf16[256,1280]{1,0:T(8,128)(2,1)}, u32[]{:S(2)}, u32[]{:S(2)}) collective-permute-start(bf16[256,1280]{1,0:T(8,128)(2,1)} %get-tuple-element.185), channel_id=1, source_target_pairs={{0,1},{1,0},{2,3},{3,2},{4,5},{5,4},{6,7},{7,6},{8,9},{9,8},{10,11... | collective-permute-start | bytes 1966088 | tf_op jit(solution)/shard_map/ppermute | solution.py:403
  328.1 37.0 %collective-permute-start.42 = (bf16[256,1280]{1,0:T(8,128)(2,1)}, bf16[256,1280]{1,0:T(8,128)(2,1)}, u32[]{:S(2)}, u32[]{:S(2)}) collective-permute-start(bf16[256,1280]{1,0:T(8,128)(2,1)} %get-tuple-element.155), channel_id=1, source_target_pairs={{0,1},{1,0},{2,3},{3,2},{4,5},{5,4},{6,7},{7,6},{8,9},{9,8},{10,11... | collective-permute-start | bytes 1966088 | tf_op jit(solution)/shard_map/ppermute | solution.py:403
  345.6 22.6 %collective-permute-start.28 = (bf16[256,1280]{1,0:T(8,128)(2,1)}, bf16[256,1280]{1,0:T(8,128)(2,1)}, u32[]{:S(2)}, u32[]{:S(2)}) collective-permute-start(bf16[256,1280]{1,0:T(8,128)(2,1)} %get-tuple-element.143), channel_id=1, source_target_pairs={{0,1},{1,0},{2,3},{3,2},{4,5},{5,4},{6,7},{7,6},{8,9},{9,8},{10,11... | collective-permute-start | bytes 1966088 | tf_op jit(solution)/shard_map/ppermute | solution.py:403
  345.7 24.3 %collective-permute-start.56 = (bf16[256,1280]{1,0:T(8,128)(2,1)}, bf16[256,1280]{1,0:T(8,128)(2,1)}, u32[]{:S(2)}, u32[]{:S(2)}) collective-permute-start(bf16[256,1280]{1,0:T(8,128)(2,1)} %get-tuple-element.171), channel_id=1, source_target_pairs={{0,1},{1,0},{2,3},{3,2},{4,5},{5,4},{6,7},{7,6},{8,9},{9,8},{10,11... | collective-permute-start | bytes 1966088 | tf_op jit(solution)/shard_map/ppermute | solution.py:403
  365.2 49.7 %collective-permute-start.69 = (bf16[128,1280]{1,0:T(8,128)(2,1)S(1)}, bf16[128,1280]{1,0:T(8,128)(2,1)S(1)}, u32[]{:S(2)}, u32[]{:S(2)}) collective-permute-start(bf16[128,1280]{1,0:T(8,128)(2,1)S(1)} %slice.611), channel_id=1, source_target_pairs={{0,2},{1,3},{2,0},{3,1},{4,6},{5,7},{6,4},{7,5},{8,10},{9,11},{10,... | collective-permute-start | bytes 983048 | tf_op jit(solution)/shard_map/ppermute | solution.py:404
  368.2 46.7 %collective-permute-start.43 = (bf16[128,1280]{1,0:T(8,128)(2,1)S(1)}, bf16[128,1280]{1,0:T(8,128)(2,1)S(1)}, u32[]{:S(2)}, u32[]{:S(2)}) collective-permute-start(bf16[128,1280]{1,0:T(8,128)(2,1)S(1)} %slice.616), channel_id=1, source_target_pairs={{0,2},{1,3},{2,0},{3,1},{4,6},{5,7},{6,4},{7,5},{8,10},{9,11},{10,... | collective-permute-start | bytes 983048 | tf_op jit(solution)/shard_map/ppermute | solution.py:404
  370.0 44.9 %collective-permute-start.29 = (bf16[128,1280]{1,0:T(8,128)(2,1)S(1)}, bf16[128,1280]{1,0:T(8,128)(2,1)S(1)}, u32[]{:S(2)}, u32[]{:S(2)}) collective-permute-start(bf16[128,1280]{1,0:T(8,128)(2,1)S(1)} %slice.618), channel_id=1, source_target_pairs={{0,2},{1,3},{2,0},{3,1},{4,6},{5,7},{6,4},{7,5},{8,10},{9,11},{10,... | collective-permute-start | bytes 983048 | tf_op jit(solution)/shard_map/ppermute | solution.py:404
  373.0 41.9 %collective-permute-start.57 = (bf16[128,1280]{1,0:T(8,128)(2,1)S(1)}, bf16[128,1280]{1,0:T(8,128)(2,1)S(1)}, u32[]{:S(2)}, u32[]{:S(2)}) collective-permute-start(bf16[128,1280]{1,0:T(8,128)(2,1)S(1)} %slice.613), channel_id=1, source_target_pairs={{0,2},{1,3},{2,0},{3,1},{4,6},{5,7},{6,4},{7,5},{8,10},{9,11},{10,... | collective-permute-start | bytes 983048 | tf_op jit(solution)/shard_map/ppermute | solution.py:404
  373.7 29.3 %collective-permute-start.45 = (bf16[128,1280]{1,0:T(8,128)(2,1)S(1)}, bf16[128,1280]{1,0:T(8,128)(2,1)S(1)}, u32[]{:S(2)}, u32[]{:S(2)}) collective-permute-start(bf16[128,1280]{1,0:T(8,128)(2,1)S(1)} %slice.615), channel_id=1, source_target_pairs={{0,2},{1,3},{2,0},{3,1},{4,6},{5,7},{6,4},{7,5},{8,10},{9,11},{10,... | collective-permute-start | bytes 983048 | tf_op jit(solution)/shard_map/ppermute | solution.py:404
  418.7 16.6 %collective-permute-start.58 = (bf16[128,1280]{1,0:T(8,128)(2,1)S(1)}, bf16[128,1280]{1,0:T(8,128)(2,1)S(1)}, u32[]{:S(2)}, u32[]{:S(2)}) collective-permute-start(bf16[128,1280]{1,0:T(8,128)(2,1)S(1)} %get-tuple-element.337), channel_id=1, source_target_pairs={{0,2},{1,3},{2,0},{3,1},{4,6},{5,7},{6,4},{7,5},{8,10},{9,11},{10,... | collective-permute-start | bytes 983048 | tf_op jit(solution)/shard_map/ppermute | solution.py:399
  453.8 218.4 %reduce-scatter.9.cloned.1.call-start = ((), (), s32[]{:S(2)}) async-start(), calls=%async_computation.9 | async-start | bytes 3686400 | tf_op jit(solution)/shard_map/reduce_scatter | solution.py:581
  469.7 254.1 %reduce-scatter.11.cloned.1.call-start = ((), (), s32[]{:S(2)}) async-start(), calls=%async_computation.10 | async-start | bytes 3686400 | tf_op jit(solution)/shard_map/reduce_scatter | solution.py:581
  487.0 310.1 %reduce-scatter.5.cloned.1.call-start = ((), (), s32[]{:S(2)}) async-start(), calls=%async_computation.7 | async-start | bytes 2949120 | tf_op jit(solution)/shard_map/reduce_scatter | solution.py:581
  500.3 29.4 %collective-permute-start.72 = (bf16[80,512]{1,0:T(8,128)(2,1)}, bf16[80,512]{1,0:T(8,128)(2,1)S(1)}, u32[]{:S(2)}, u32[]{:S(2)}) collective-permute-start(bf16[80,512]{1,0:T(8,128)(2,1)} %get-tuple-element.189), channel_id=1, source_target_pairs={{0,4},{4,8},{8,12},{12,0},{1,5},{5,9},{9,13},{13,1},{2,6},{6,10},{... | collective-permute-start | bytes 245768 | tf_op jit(solution)/shard_map/ppermute | solution.py:407
  500.3 31.8 %collective-permute-start.73 = (bf16[80,512]{1,0:T(8,128)(2,1)S(1)}, bf16[80,512]{1,0:T(8,128)(2,1)S(1)}, u32[]{:S(2)}, u32[]{:S(2)}) collective-permute-start(bf16[80,512]{1,0:T(8,128)(2,1)S(1)} %copy-done.79), channel_id=1, source_target_pairs={{0,8},{4,12},{8,0},{12,4},{1,9},{5,13},{9,1},{13,5},{2,10},{6,14},... | collective-permute-start | bytes 245768 | tf_op jit(solution)/shard_map/ppermute | solution.py:407
  502.2 29.9 %collective-permute-start.74 = (bf16[80,512]{1,0:T(8,128)(2,1)S(1)}, bf16[80,512]{1,0:T(8,128)(2,1)S(1)}, u32[]{:S(2)}, u32[]{:S(2)}) collective-permute-start(bf16[80,512]{1,0:T(8,128)(2,1)S(1)} %copy-done.78), channel_id=1, source_target_pairs={{0,12},{4,0},{8,4},{12,8},{1,13},{5,1},{9,5},{13,9},{2,14},{6,2},{... | collective-permute-start | bytes 245768 | tf_op jit(solution)/shard_map/ppermute | solution.py:407
  507.8 43.0 %collective-permute-start.60 = (bf16[80,512]{1,0:T(8,128)(2,1)S(1)}, bf16[80,512]{1,0:T(8,128)(2,1)S(1)}, u32[]{:S(2)}, u32[]{:S(2)}) collective-permute-start(bf16[80,512]{1,0:T(8,128)(2,1)S(1)} %copy-done.77), channel_id=1, source_target_pairs={{0,4},{4,8},{8,12},{12,0},{1,5},{5,9},{9,13},{13,1},{2,6},{6,10},{... | collective-permute-start | bytes 245768 | tf_op jit(solution)/shard_map/ppermute | solution.py:407
  507.8 46.8 %collective-permute-start.61 = (bf16[80,512]{1,0:T(8,128)(2,1)S(1)}, bf16[80,512]{1,0:T(8,128)(2,1)S(1)}, u32[]{:S(2)}, u32[]{:S(2)}) collective-permute-start(bf16[80,512]{1,0:T(8,128)(2,1)S(1)} %copy-done.76), channel_id=1, source_target_pairs={{0,8},{4,12},{8,0},{12,4},{1,9},{5,13},{9,1},{13,5},{2,10},{6,14},... | collective-permute-start | bytes 245768 | tf_op jit(solution)/shard_map/ppermute | solution.py:407
  529.7 26.0 %collective-permute-start.62 = (bf16[80,512]{1,0:T(8,128)(2,1)S(1)}, bf16[80,512]{1,0:T(8,128)(2,1)}, u32[]{:S(2)}, u32[]{:S(2)}) collective-permute-start(bf16[80,512]{1,0:T(8,128)(2,1)S(1)} %copy-done.75), channel_id=1, source_target_pairs={{0,12},{4,0},{8,4},{12,8},{1,13},{5,1},{9,5},{13,9},{2,14},{6,2},{... | collective-permute-start | bytes 245768 | tf_op jit(solution)/shard_map/ppermute | solution.py:407
  532.1 24.5 %collective-permute-start.51 = (bf16[240,512]{1,0:T(8,128)(2,1)}, bf16[240,512]{1,0:T(8,128)(2,1)S(1)}, u32[]{:S(2)}, u32[]{:S(2)}) collective-permute-start(bf16[240,512]{1,0:T(8,128)(2,1)} %get-tuple-element.165), channel_id=1, source_target_pairs={{0,4},{4,8},{8,12},{12,0},{1,5},{5,9},{9,13},{13,1},{2,6},{6,10},{... | collective-permute-start | bytes 737288 | tf_op jit(solution)/shard_map/ppermute | solution.py:407
  532.1 44.4 %collective-permute-start.52 = (bf16[240,512]{1,0:T(8,128)(2,1)}, bf16[240,512]{1,0:T(8,128)(2,1)S(1)}, u32[]{:S(2)}, u32[]{:S(2)}) collective-permute-start(bf16[240,512]{1,0:T(8,128)(2,1)} %get-tuple-element.166), channel_id=1, source_target_pairs={{0,8},{4,12},{8,0},{12,4},{1,9},{5,13},{9,1},{13,5},{2,10},{6,14},... | collective-permute-start | bytes 737288 | tf_op jit(solution)/shard_map/ppermute | solution.py:407
  550.8 25.9 %collective-permute-start.53 = (bf16[240,512]{1,0:T(8,128)(2,1)S(1)}, bf16[240,512]{1,0:T(8,128)(2,1)}, u32[]{:S(2)}, u32[]{:S(2)}) collective-permute-start(bf16[240,512]{1,0:T(8,128)(2,1)S(1)} %copy-done.64), channel_id=1, source_target_pairs={{0,12},{4,0},{8,4},{12,8},{1,13},{5,1},{9,5},{13,9},{2,14},{6,2},{... | collective-permute-start | bytes 737288 | tf_op jit(solution)/shard_map/ppermute | solution.py:407
  555.3 33.2 %collective-permute-start.75 = (bf16[240,512]{1,0:T(8,128)(2,1)}, bf16[240,512]{1,0:T(8,128)(2,1)S(1)}, u32[]{:S(2)}, u32[]{:S(2)}) collective-permute-start(bf16[240,512]{1,0:T(8,128)(2,1)} %get-tuple-element.193), channel_id=1, source_target_pairs={{0,4},{4,8},{8,12},{12,0},{1,5},{5,9},{9,13},{13,1},{2,6},{6,10},{... | collective-permute-start | bytes 737288 | tf_op jit(solution)/shard_map/ppermute | solution.py:407
  555.7 53.6 %collective-permute-start.76 = (bf16[240,512]{1,0:T(8,128)(2,1)}, bf16[240,512]{1,0:T(8,128)(2,1)S(1)}, u32[]{:S(2)}, u32[]{:S(2)}) collective-permute-start(bf16[240,512]{1,0:T(8,128)(2,1)} %get-tuple-element.194), channel_id=1, source_target_pairs={{0,8},{4,12},{8,0},{12,4},{1,9},{5,13},{9,1},{13,5},{2,10},{6,14},... | collective-permute-start | bytes 737288 | tf_op jit(solution)/shard_map/ppermute | solution.py:407
  556.6 53.4 %collective-permute-start.77 = (bf16[240,512]{1,0:T(8,128)(2,1)}, bf16[240,512]{1,0:T(8,128)(2,1)}, u32[]{:S(2)}, u32[]{:S(2)}) collective-permute-start(bf16[240,512]{1,0:T(8,128)(2,1)} %get-tuple-element.195), channel_id=1, source_target_pairs={{0,12},{4,0},{8,4},{12,8},{1,13},{5,1},{9,5},{13,9},{2,14},{6,2},{... | collective-permute-start | bytes 737288 | tf_op jit(solution)/shard_map/ppermute | solution.py:407
  576.5 40.4 %collective-permute-start.63 = (bf16[240,512]{1,0:T(8,128)(2,1)}, bf16[240,512]{1,0:T(8,128)(2,1)S(1)}, u32[]{:S(2)}, u32[]{:S(2)}) collective-permute-start(bf16[240,512]{1,0:T(8,128)(2,1)} %get-tuple-element.179), channel_id=1, source_target_pairs={{0,4},{4,8},{8,12},{12,0},{1,5},{5,9},{9,13},{13,1},{2,6},{6,10},{... | collective-permute-start | bytes 737288 | tf_op jit(solution)/shard_map/ppermute | solution.py:407
  576.8 43.1 %collective-permute-start.64 = (bf16[240,512]{1,0:T(8,128)(2,1)}, bf16[240,512]{1,0:T(8,128)(2,1)S(1)}, u32[]{:S(2)}, u32[]{:S(2)}) collective-permute-start(bf16[240,512]{1,0:T(8,128)(2,1)} %get-tuple-element.180), channel_id=1, source_target_pairs={{0,8},{4,12},{8,0},{12,4},{1,9},{5,13},{9,1},{13,5},{2,10},{6,14},... | collective-permute-start | bytes 737288 | tf_op jit(solution)/shard_map/ppermute | solution.py:407
  588.5 31.4 %collective-permute-start.65 = (bf16[240,512]{1,0:T(8,128)(2,1)}, bf16[240,512]{1,0:T(8,128)(2,1)}, u32[]{:S(2)}, u32[]{:S(2)}) collective-permute-start(bf16[240,512]{1,0:T(8,128)(2,1)} %get-tuple-element.181), channel_id=1, source_target_pairs={{0,12},{4,0},{8,4},{12,8},{1,13},{5,1},{9,5},{13,9},{2,14},{6,2},{... | collective-permute-start | bytes 737288 | tf_op jit(solution)/shard_map/ppermute | solution.py:407
  610.0 29.1 %collective-permute-start.54 = (bf16[256,1280]{1,0:T(8,128)(2,1)}, bf16[256,1280]{1,0:T(8,128)(2,1)S(1)}, u32[]{:S(2)}, u32[]{:S(2)}) collective-permute-start(bf16[256,1280]{1,0:T(8,128)(2,1)} %get-tuple-element.169), channel_id=1, source_target_pairs={{0,1},{1,0},{2,3},{3,2},{4,5},{5,4},{6,7},{7,6},{8,9},{9,8},{10,11... | collective-permute-start | bytes 1966088 | tf_op jit(solution)/shard_map/ppermute | solution.py:403
  616.3 25.0 %collective-permute-start.78 = (bf16[256,1280]{1,0:T(8,128)(2,1)}, bf16[256,1280]{1,0:T(8,128)(2,1)}, u32[]{:S(2)}, u32[]{:S(2)}) collective-permute-start(bf16[256,1280]{1,0:T(8,128)(2,1)} %get-tuple-element.197), channel_id=1, source_target_pairs={{0,1},{1,0},{2,3},{3,2},{4,5},{5,4},{6,7},{7,6},{8,9},{9,8},{10,11... | collective-permute-start | bytes 1966088 | tf_op jit(solution)/shard_map/ppermute | solution.py:403
  626.9 16.7 %collective-permute-start.66 = (bf16[256,1280]{1,0:T(8,128)(2,1)}, bf16[256,1280]{1,0:T(8,128)(2,1)}, u32[]{:S(2)}, u32[]{:S(2)}) collective-permute-start(bf16[256,1280]{1,0:T(8,128)(2,1)} %get-tuple-element.183), channel_id=1, source_target_pairs={{0,1},{1,0},{2,3},{3,2},{4,5},{5,4},{6,7},{7,6},{8,9},{9,8},{10,11... | collective-permute-start | bytes 1966088 | tf_op jit(solution)/shard_map/ppermute | solution.py:403
  639.1 293.4 %all-reduce.3.cloned.1.call-start = ((), (), s32[]{:S(2)}) async-start(), calls=%async_computation.11 | async-start | bytes 188416 | tf_op jit(solution)/shard_map/psum | solution.py:605
  642.7 14.7 %collective-permute-start.79 = (bf16[128,1280]{1,0:T(8,128)(2,1)S(1)}, bf16[128,1280]{1,0:T(8,128)(2,1)S(1)}, u32[]{:S(2)}, u32[]{:S(2)}) collective-permute-start(bf16[128,1280]{1,0:T(8,128)(2,1)S(1)} %slice.610), channel_id=1, source_target_pairs={{0,2},{1,3},{2,0},{3,1},{4,6},{5,7},{6,4},{7,5},{8,10},{9,11},{10,... | collective-permute-start | bytes 983048 | tf_op jit(solution)/shard_map/ppermute | solution.py:404
  644.9 19.1 %collective-permute-start.67 = (bf16[128,1280]{1,0:T(8,128)(2,1)S(1)}, bf16[128,1280]{1,0:T(8,128)(2,1)S(1)}, u32[]{:S(2)}, u32[]{:S(2)}) collective-permute-start(bf16[128,1280]{1,0:T(8,128)(2,1)S(1)} %slice.612), channel_id=1, source_target_pairs={{0,2},{1,3},{2,0},{3,1},{4,6},{5,7},{6,4},{7,5},{8,10},{9,11},{10,... | collective-permute-start | bytes 983048 | tf_op jit(solution)/shard_map/ppermute | solution.py:404
  (119 other events, 867.6 us)
Sparse Core Ops, SparseCore 0:
  12.0 66.6 all-gather.3
  80.8 110.8 all-gather.5
  193.8 73.1 all-gather.7
  454.0 68.0 reduce-scatter.6
  525.5 119.3 reduce-scatter.8
  648.3 75.4 reduce-scatter.10
  727.3 69.7 reduce-scatter.4
  805.2 127.2 all-reduce.2
